TPU v7x, 32 devices: a whole 2x2x4 slice. The times are simulated.
32 devices in a mesh: seq: 16 (over z, y, x), head: 2 (over core).
Axes of the slice: x: 2, y: 2, z: 4, core: 2. Of those that a mesh axis runs over, the one named last changes fastest.
Arguments:
- queries: bfloat16 [4096, 4096], P('seq', 'head'), may hold values from -1.796875 to 1.796875
- key_rows: bfloat16 [4096, 4096], P('seq', 'head'), may hold values from -1.796875 to 1.796875
- values: bfloat16 [4096, 4096], P('seq', 'head'), may hold values from -100 to 100
- out_weight: bfloat16 [4096, 4096], P('head', 'seq'), may hold values from -0.125 to 0.125
- out_grad: bfloat16 [4096, 4096], P('seq', 'head'), may hold values from -6 to 6
Outputs:
- mixed: bfloat16 [4096, 4096], P('seq', 'head')
- query_grad: bfloat16 [4096, 4096], P('seq', 'head')
- key_grad: bfloat16 [4096, 4096], P('seq', 'head')
- value_grad: bfloat16 [4096, 4096], P('seq', 'head')
All inputs are finite; a program needn't handle non-finite values.
Results may differ from a plain program's by a relative error of at most 0.014.
Values may be sent and summed in bfloat16 or wider, within the bound.
A program may use at most 128 MiB of HBM per device.

v0:
```python
import functools

import jax
import jax.numpy as jnp
from jax import lax
from jax.experimental import pallas as pl
from jax.experimental.pallas import tpu as pltpu
from jax.sharding import PartitionSpec as P

HEAD_DIM = 128
MESH = pl.DeviceIdType.MESH
PLANE = 4


def prefix_2(value, axis, combine, identity):
    length, position = (lax.axis_size(axis), lax.axis_index(axis))
    everything = lax.all_gather(value, axis)
    start = jnp.broadcast_to(jnp.asarray(identity, value.dtype), value.shape)

    def hop(k, before):
        reached = k < position
        new = combine(before, everything[k])
        return jnp.where(reached, new, before)

    return lax.fori_loop(0, length, hop, start)


def prefix_3(value, axis, combine, identity):
    length, position = (lax.axis_size(axis), lax.axis_index(axis))
    everything = lax.all_gather(value.astype(jnp.bfloat16), axis)
    start = jnp.broadcast_to(jnp.asarray(identity, value.dtype), value.shape)

    def hop(k, before):
        at = length - 1 - k
        reached = at > position
        new = combine(before, everything[at].astype(value.dtype))
        return jnp.where(reached, new, before)

    return lax.fori_loop(0, length, hop, start)


def lower_mask(length):
    row_ids = lax.broadcasted_iota(jnp.int32, (length, length), 0)
    col_ids = lax.broadcasted_iota(jnp.int32, (length, length), 1)
    return row_ids >= col_ids


def add_states(earlier, latter):
    return earlier + latter


def contract_cols(left_side, right_side):
    return lax.dot_general(
        left_side, right_side, (((1,), (1,)), ((), ())), preferred_element_type=jnp.float32
    )


def contract_rows(left_side, right_side):
    return lax.dot_general(
        left_side, right_side, (((0,), (0,)), ((), ())), preferred_element_type=jnp.float32
    )


def contract_mid(left_side, right_side):
    return jnp.dot(left_side, right_side, preferred_element_type=jnp.float32)


def per_device(queries, key_rows, values, out_weight, out_grad):
    length = queries.shape[0]
    heads_here = queries.shape[1] // HEAD_DIM
    query_heads = queries.reshape(length, heads_here, HEAD_DIM)
    key_heads = key_rows.reshape(length, heads_here, HEAD_DIM)
    value_heads = values.reshape(length, heads_here, HEAD_DIM)
    causal = lower_mask(length)[None]
    local_state = jnp.einsum(
        "shd,she->hde", key_heads, value_heads, preferred_element_type=jnp.float32
    )
    prefix = prefix_2(local_state, "seq", add_states, jnp.zeros_like(local_state))
    prefix_low = prefix.astype(jnp.bfloat16)
    scores = jnp.einsum("thd,shd->hts", query_heads, key_heads, preferred_element_type=jnp.float32)
    weights = jnp.where(causal, scores, 0.0).astype(jnp.bfloat16)
    numerator = jnp.einsum("hts,she->the", weights, value_heads, preferred_element_type=jnp.float32)
    numerator = numerator + jnp.einsum(
        "thd,hde->the", query_heads, prefix_low, preferred_element_type=jnp.float32
    )
    spread = jnp.sqrt(jnp.mean(numerator * numerator, axis=-1, keepdims=True) + 1e-06)
    normed = numerator / spread
    attended = normed.astype(jnp.bfloat16).reshape(length, heads_here * HEAD_DIM)
    full_weight = lax.all_gather(out_weight, "seq", axis=1, tiled=True)
    partial_value = jnp.dot(attended, full_weight, preferred_element_type=jnp.float32)
    layer_out = lax.psum_scatter(
        partial_value.astype(jnp.bfloat16), "head", scatter_dimension=1, tiled=True
    )
    out_dir = contract_cols(lax.all_gather(out_grad, "head", axis=1, tiled=True), full_weight)
    out_dir = out_dir.reshape(length, heads_here, HEAD_DIM)
    along_dir = jnp.mean(out_dir * normed, axis=-1, keepdims=True)
    numer_grad = ((out_dir - normed * along_dir) / spread).astype(jnp.bfloat16)
    local_grad = jnp.einsum(
        "thd,the->hde", query_heads, numer_grad, preferred_element_type=jnp.float32
    )
    suffix = prefix_3(local_grad, "seq", add_states, jnp.zeros_like(local_grad))
    suffix_low = suffix.astype(jnp.bfloat16)
    pair_scores = jnp.einsum(
        "the,she->hts", numer_grad, value_heads, preferred_element_type=jnp.float32
    )
    pair_low = jnp.where(causal, pair_scores, 0.0).astype(jnp.bfloat16)
    query_out = jnp.einsum("hts,shd->thd", pair_low, key_heads, preferred_element_type=jnp.float32)
    query_out = query_out + jnp.einsum(
        "the,hde->thd", numer_grad, prefix_low, preferred_element_type=jnp.float32
    )
    key_out = jnp.einsum("hts,thd->shd", pair_low, query_heads, preferred_element_type=jnp.float32)
    key_out = key_out + jnp.einsum(
        "she,hde->shd", value_heads, suffix_low, preferred_element_type=jnp.float32
    )
    value_out = jnp.einsum("hts,the->she", weights, numer_grad, preferred_element_type=jnp.float32)
    value_out = value_out + jnp.einsum(
        "shd,hde->she", key_heads, suffix_low, preferred_element_type=jnp.float32
    )
    flat_shape = (length, heads_here * HEAD_DIM)
    return (
        layer_out,
        query_out.reshape(flat_shape).astype(jnp.bfloat16),
        key_out.reshape(flat_shape).astype(jnp.bfloat16),
        value_out.reshape(flat_shape).astype(jnp.bfloat16),
    )


def visit_tables(planes):
    half, rows = planes // 2, []
    for own in range(planes):
        rows.append(sorted(range(planes), key=lambda other: (other // half != own // half, abs(other - own))))
    return rows


def pick(table, position):
    found = jnp.int32(table[0])
    for at in range(1, len(table)):
        found = jnp.where(position == at, jnp.int32(table[at]), found)
    return found


def kernel(
    blocks, q_in, k_in, v_in, w_ref, g_ref,
    mixed_ref, dq_ref, dk_ref, dv_ref,
    q_ref, k_ref, v_ref, w_all, g_all, st_send, st_recv, pre_send, prefix, lg_send, lg_recv, suf_send, suffix,
    out_dir, normed, inv_spread, weights, attended, p_own, p_send, p_recv, ng, k_part, v_part,
    x_send, x_recv,
    w_recv_sem, wx_sem, wy_sem, wz_sem, local_sem, g_sem, a_send_sem, a_recv_sem, p_send_sem, p_recv_sem,
    x_send_sem, x_recv_sem,
):
    me = lax.axis_index("seq")
    core = lax.axis_index("head")
    other = 1 - core
    planes = blocks // PLANE
    half_planes = planes // 2
    size = blocks // 2
    share = st_send.shape[0] // size
    team, rank = me // size, lax.rem(me, size)
    spot = lax.rem(me, PLANE)
    level = me // PLANE
    bit_x, bit_y = lax.rem(spot, 2), spot // 2
    spot_x = spot + 1 - 2 * bit_x
    spot_y = spot + 2 - 4 * bit_y
    spot_d = spot_x + 2 - 4 * bit_y
    length, width = q_ref.shape
    heads = width // HEAD_DIM
    rows, cols = w_ref.shape
    half = rows // 2
    per_core = blocks // 2

    def at_seq(position):
        return (position, core)

    nbr_x = level * PLANE + spot_x
    nbr_y = level * PLANE + spot_y

    q_load = pltpu.make_async_copy(q_in, q_ref, local_sem.at[2])
    k_load = pltpu.make_async_copy(k_in, k_ref, local_sem.at[3])
    v_load = pltpu.make_async_copy(v_in, v_ref, local_sem.at[4])
    k_load.start()
    v_load.start()
    barrier = pltpu.get_barrier_semaphore()

    def greet(i, carry):
        pl.semaphore_signal(barrier, inc=1, device_id=at_seq(lax.rem(me + i, blocks)), device_id_type=MESH)
        return carry

    lax.fori_loop(1, blocks, greet, 0)
    pl.semaphore_signal(barrier, inc=1, device_id=(me, other), device_id_type=MESH)

    own_w = pltpu.make_async_copy(w_ref, w_all.at[me], local_sem.at[0])
    own_g = pltpu.make_async_copy(g_ref, g_all.at[core], local_sem.at[1])
    q_load.start()
    own_w.start()
    own_g.start()
    k_load.wait()
    v_load.wait()

    def head_cols(h):
        return pl.ds(pl.multiple_of(h * HEAD_DIM, HEAD_DIM), HEAD_DIM)

    def make_state(h, carry):
        c = head_cols(h)
        st_send[h] = contract_rows(k_ref[:, c], v_ref[:, c]).astype(jnp.bfloat16)
        return carry

    lax.fori_loop(0, heads, make_state, 0)
    st_recv[rank] = st_send[pl.ds(rank * share, share)]

    pl.semaphore_wait(barrier, blocks)

    def state_copy(src, dst, kind, peer):
        return pltpu.make_async_remote_copy(
            src_ref=src(peer), dst_ref=dst(rank),
            send_sem=a_send_sem.at[kind, peer], recv_sem=a_recv_sem.at[kind, rank],
            device_id=at_seq(team * size + peer), device_id_type=MESH,
        )

    def leave(src, dst, kind, peer):
        @pl.when(peer != rank)
        def _():
            state_copy(src, dst, kind, peer).start()

    def exchange(src, dst, kind, start):
        def one(i, carry):
            copy = state_copy(src, dst, kind, lax.rem(rank + i, size))
            copy.start() if start else copy.wait_send()
            return carry

        lax.fori_loop(1, size, one, 0)

    def arrived(src, dst, kind):
        def one(i, carry):
            peer = lax.rem(rank + i, size)
            pltpu.make_async_remote_copy(
                src_ref=src(rank), dst_ref=dst(peer),
                send_sem=a_send_sem.at[kind, rank], recv_sem=a_recv_sem.at[kind, peer],
                device_id=at_seq(team * size + peer), device_id_type=MESH,
            ).wait_recv()
            return carry

        lax.fori_loop(1, size, one, 0)

    def pair_of(ref):
        return lambda owner: ref.at[pl.ds(owner * share, share)]

    def slot_of(ref):
        return lambda owner: ref.at[owner]

    def team_total(kind):
        return pltpu.make_async_remote_copy(
            src_ref=x_send.at[kind], dst_ref=x_recv.at[kind],
            send_sem=x_send_sem.at[kind], recv_sem=x_recv_sem.at[kind],
            device_id=at_seq((1 - team) * size + rank), device_id_type=MESH,
        )

    def running(first_team, kind, source, low_send, low_own, backwards):
        @pl.when(team == first_team)
        def _():
            x_recv[kind] = jnp.zeros(x_recv.shape[1:], jnp.float32)

        @pl.when(team != first_team)
        def _():
            team_total(kind).wait_recv()

        def one(i, total):
            at = size - 1 - i if backwards else i
            low_send[at] = total.astype(jnp.bfloat16)
            return total + source[at].astype(jnp.float32)

        x_send[kind] = lax.fori_loop(0, size, one, x_recv[kind])
        low_own[pl.ds(rank * share, share)] = low_send[rank]

        @pl.when(team == first_team)
        def _():
            team_total(kind).start()

    g_copy = pltpu.make_async_remote_copy(
        src_ref=g_ref, dst_ref=g_all.at[core], send_sem=g_sem.at[0], recv_sem=g_sem.at[1],
        device_id=(me, other), device_id_type=MESH,
    )
    g_copy.start()
    exchange(pair_of(st_send), slot_of(st_recv), 0, True)

    def piece(block, part, sems, target, own=False):
        span = pl.ds(part * half, half)
        return pltpu.make_async_remote_copy(
            src_ref=w_ref.at[span] if own else w_all.at[block, span],
            dst_ref=w_all.at[block, span],
            send_sem=sems.at[block, part], recv_sem=w_recv_sem.at[block, part],
            device_id=at_seq(target), device_id_type=MESH,
        )

    up_ok = level + 1 < planes
    down_ok = level > 0
    up = jnp.minimum(me + PLANE, blocks - PLANE + spot)
    down = jnp.maximum(me - PLANE, spot)

    for part in range(2):
        piece(me, part, wx_sem, nbr_x, True).start()
        piece(me, part, wy_sem, nbr_y, True).start()

        @pl.when(up_ok)
        def _():
            piece(me, part, wz_sem.at[0], up, True).start()

        @pl.when(down_ok)
        def _():
            piece(me, part, wz_sem.at[1], down, True).start()

    tables = visit_tables(planes)
    order = [pick([tables[z][k] for z in range(planes)], level) for k in range(planes)]

    def passing(k):
        return jnp.where(order[k] < level, up_ok, down_ok)

    def along_z(k, where, finish=False):
        plane = order[k]
        block = plane * PLANE + where
        going_up = plane < level
        for part in range(2):
            for sems, way, go in ((wz_sem.at[0], up, going_up), (wz_sem.at[1], down, jnp.logical_not(going_up))):

                @pl.when(jnp.logical_and(go, passing(k)))
                def _():
                    copy = piece(block, part, sems, way)
                    if finish:
                        copy.wait_send()
                    else:
                        copy.wait_recv()
                        copy.start()

    def end_of_z(k, where, part):
        @pl.when(jnp.logical_not(passing(k)))
        def _():
            piece(order[k] * PLANE + where, part, wx_sem, nbr_x).wait_recv()

    def across(k, finish=False):
        block = order[k] * PLANE + spot
        for part in range(2):
            if not finish:
                end_of_z(k, spot, part)
            for copy in (piece(block, part, wx_sem, nbr_x), piece(block, part, wy_sem, nbr_y)):
                copy.wait_send() if finish else copy.start()

    def relay_step(k, finish=False):
        plane = order[k]
        to_x = piece(plane * PLANE + spot_y, 0, wx_sem, nbr_x)
        to_y = piece(plane * PLANE + spot_x, 1, wy_sem, nbr_y)
        for copy in (to_x, to_y):
            if finish:
                copy.wait_send()
            else:
                copy.wait_recv()
                copy.start()

    def cross_step(k, finish=False):
        block = order[k] * PLANE + spot_d
        for part in range(2):

            @pl.when(level == half_planes - 1)
            def _():
                copy = piece(block, part, wz_sem.at[0], up)
                copy.wait_send() if finish else copy.start()

            @pl.when(level == half_planes)
            def _():
                copy = piece(block, part, wz_sem.at[1], down)
                copy.wait_send() if finish else copy.start()

    def settle(k):
        plane = order[k]
        near = ((spot_y, 1), (spot_x, 0), (spot_d, 0), (spot_d, 1))
        far = ((spot_y, 0), (spot_x, 0), (spot_y, 1), (spot_x, 1))
        for where, part in near if k < half_planes else far:
            piece(plane * PLANE + where, part, wx_sem, nbr_x).wait_recv()
        if k >= half_planes:
            for part in range(2):
                end_of_z(k, spot_d, part)

    causal = lower_mask(length)

    def score_step(h, carry):
        c = head_cols(h)
        kept = jnp.where(causal, contract_cols(q_ref[:, c], k_ref[:, c]), 0.0).astype(jnp.bfloat16)
        weights[h] = kept
        normed[h] = contract_mid(kept, v_ref[:, c])
        return carry

    def norm_step(h, carry):
        c = head_cols(h)
        numerator = normed[h] + contract_mid(q_ref[:, c], prefix[h])
        inv = 1.0 / jnp.sqrt(jnp.mean(numerator * numerator, axis=-1, keepdims=True) + 1e-06)
        value = numerator * inv
        normed[h] = value
        inv_spread[h] = jnp.broadcast_to(inv, (length, HEAD_DIM))
        attended[:, c] = value.astype(jnp.bfloat16)
        return carry

    tile = cols
    n_tiles = rows // tile

    def grad_cols(block):
        return g_all[block // per_core, :, pl.ds(pl.multiple_of(lax.rem(block, per_core) * cols, cols), cols)]

    def direction_step(k):
        base = order[k] * PLANE

        def one(n, carry):
            span = pl.ds(pl.multiple_of(n * tile, tile), tile)
            total = contract_cols(grad_cols(base), w_all[base, span])
            for s in range(1, PLANE):
                total = total + contract_cols(grad_cols(base + s), w_all[base + s, span])
            if k > 0:
                total = total + out_dir[:, span]
            out_dir[:, span] = total
            return carry

        lax.fori_loop(0, n_tiles, one, 0)

    def p_copy(slot):
        return pltpu.make_async_remote_copy(
            src_ref=p_send.at[slot], dst_ref=p_recv.at[slot],
            send_sem=p_send_sem.at[slot], recv_sem=p_recv_sem.at[slot],
            device_id=(me, other), device_id_type=MESH,
        )

    def partial_step(k):
        def one(s, carry):
            block = order[k] * PLANE + s
            term = contract_mid(attended[...], w_all[block]).astype(jnp.bfloat16)
            slot = lax.rem(block, per_core)

            @pl.when(block // per_core == core)
            def _():
                p_own[slot] = term

            @pl.when(block // per_core != core)
            def _():
                p_send[slot] = term
                p_copy(slot).start()

            return carry

        lax.fori_loop(0, PLANE, one, 0)

    q_load.wait()
    lax.fori_loop(0, heads, score_step, 0)
    relay_step(0)
    along_z(1, spot)
    across(1)
    along_z(2, spot)
    arrived(pair_of(st_send), slot_of(st_recv), 0)
    running(0, 0, st_recv, pre_send, prefix, False)
    exchange(slot_of(pre_send), pair_of(prefix), 1, True)
    settle(0)
    cross_step(0)
    along_z(3, spot)
    relay_step(1)
    across(2)
    own_w.wait()
    own_g.wait()
    g_copy.wait()
    direction_step(0)
    along_z(2, spot_d)
    settle(1)
    cross_step(1)
    across(3)
    direction_step(1)
    arrived(slot_of(pre_send), pair_of(prefix), 1)
    lax.fori_loop(0, heads, norm_step, 0)
    partial_step(0)
    along_z(3, spot_d)
    partial_step(1)
    settle(2)
    direction_step(2)
    partial_step(2)
    settle(3)
    direction_step(3)

    def numer_step(h, carry):
        c = head_cols(h)
        toward, unit = out_dir[:, c], normed[h]
        along = jnp.mean(toward * unit, axis=-1, keepdims=True)
        low = ((toward - unit * along) * inv_spread[h]).astype(jnp.bfloat16)
        ng[:, c] = low
        lg_send[h] = contract_rows(q_ref[:, c], low).astype(jnp.bfloat16)

        @pl.when(jnp.logical_and(h > 0, lax.rem(h, share) == 0))
        def _():
            leave(pair_of(lg_send), slot_of(lg_recv), 2, h // share - 1)

        return carry

    lax.fori_loop(0, heads, numer_step, 0)
    leave(pair_of(lg_send), slot_of(lg_recv), 2, size - 1)
    lg_recv[rank] = lg_send[pl.ds(rank * share, share)]
    partial_step(planes - 1)
    arrived(pair_of(lg_send), slot_of(lg_recv), 2)
    running(1, 1, lg_recv, suf_send, suffix, True)
    exchange(slot_of(suf_send), pair_of(suffix), 3, True)

    def pair_step(h, carry):
        c = head_cols(h)
        low = ng[:, c]
        pair = jnp.where(causal, contract_cols(low, v_ref[:, c]), 0.0).astype(jnp.bfloat16)
        dq_ref[:, c] = (contract_mid(pair, k_ref[:, c]) + contract_cols(low, prefix[h])).astype(jnp.bfloat16)
        k_part[h] = contract_rows(pair, q_ref[:, c])
        v_part[h] = contract_rows(weights[h], low)
        return carry

    lax.fori_loop(0, heads, pair_step, 0)

    def mix_step(slot, carry):
        p_copy(slot).wait()
        c = pl.ds(pl.multiple_of(slot * cols, cols), cols)
        mixed_ref[:, c] = (p_own[slot].astype(jnp.float32) + p_recv[slot].astype(jnp.float32)).astype(jnp.bfloat16)
        return carry

    lax.fori_loop(0, per_core, mix_step, 0)
    arrived(slot_of(suf_send), pair_of(suffix), 3)

    def last_step(h, carry):
        c = head_cols(h)
        dk_ref[:, c] = (k_part[h] + contract_cols(v_ref[:, c], suffix[h])).astype(jnp.bfloat16)
        dv_ref[:, c] = (v_part[h] + contract_mid(k_ref[:, c], suffix[h])).astype(jnp.bfloat16)
        return carry

    lax.fori_loop(0, heads, last_step, 0)

    for part in range(2):
        piece(me, part, wx_sem, nbr_x, True).wait_send()
        piece(me, part, wy_sem, nbr_y, True).wait_send()

        @pl.when(up_ok)
        def _():
            piece(me, part, wz_sem.at[0], up, True).wait_send()

        @pl.when(down_ok)
        def _():
            piece(me, part, wz_sem.at[1], down, True).wait_send()

    for k in range(1, planes):
        along_z(k, spot, True)
        across(k, True)
    for k in range(half_planes):
        relay_step(k, True)
        cross_step(k, True)
    for k in range(half_planes, planes):
        along_z(k, spot_d, True)
    exchange(pair_of(st_send), slot_of(st_recv), 0, False)
    exchange(slot_of(pre_send), pair_of(prefix), 1, False)
    exchange(pair_of(lg_send), slot_of(lg_recv), 2, False)
    exchange(slot_of(suf_send), pair_of(suffix), 3, False)
    for kind in range(2):

        @pl.when(team == kind)
        def _():
            team_total(kind).wait_send()


def store_kernel(*refs):
    count = (len(refs) - 1) // 2
    copies = [pltpu.make_async_copy(refs[i], refs[count + i], refs[-1].at[i]) for i in range(count)]
    for copy in copies:
        copy.start()
    for copy in copies:
        copy.wait()


def store(*arrays):
    count = len(arrays)
    return pl.pallas_call(
        store_kernel,
        out_shape=tuple(jax.ShapeDtypeStruct(a.shape, a.dtype) for a in arrays),
        in_specs=[pl.BlockSpec(memory_space=pltpu.VMEM)] * count,
        out_specs=(pl.BlockSpec(memory_space=pltpu.HBM),) * count,
        scratch_shapes=[pltpu.SemaphoreType.DMA((count,))],
        compiler_params=pltpu.CompilerParams(vmem_limit_bytes=8 * 2**20),
    )(*arrays)


def fused(blocks, queries, key_rows, values, out_weight, out_grad):
    length, width = queries.shape
    heads = width // HEAD_DIM
    rows, cols = out_weight.shape
    per_core = blocks // 2
    low, wide = jnp.bfloat16, jnp.float32
    size = blocks // 2
    share = heads // size
    state = pltpu.VMEM((heads, HEAD_DIM, HEAD_DIM), low)
    slots = pltpu.VMEM((size, share, HEAD_DIM, HEAD_DIM), low)
    totals = pltpu.VMEM((2, share, HEAD_DIM, HEAD_DIM), wide)
    by_head = pltpu.VMEM((heads, length, HEAD_DIM), wide)
    flat = pltpu.VMEM((length, width), low)
    parts = pltpu.VMEM((per_core, length, cols), low)
    dma = pltpu.SemaphoreType.DMA
    out = jax.ShapeDtypeStruct((length, width), low)
    vmem, in_hbm = pl.BlockSpec(memory_space=pltpu.VMEM), pl.BlockSpec(memory_space=pltpu.HBM)
    results = pl.pallas_call(
        functools.partial(kernel, blocks),
        out_shape=(out, out, out, out),
        in_specs=[in_hbm] * 5,
        out_specs=(vmem, vmem, vmem, vmem),
        scratch_shapes=[
            flat, flat, flat,
            pltpu.VMEM((blocks, rows, cols), low),
            pltpu.VMEM((2, length, width), low),
            state, slots, slots, state, state, slots, slots, state,
            pltpu.VMEM((length, rows), wide),
            by_head, by_head,
            pltpu.VMEM((heads, length, length), low),
            flat, parts, parts, parts, flat, by_head, by_head,
            totals, totals,
            dma((blocks, 2)), dma((blocks, 2)), dma((blocks, 2)), dma((2, blocks, 2)),
            dma((5,)), dma((2,)), dma((4, blocks)), dma((4, blocks)), dma((per_core,)), dma((per_core,)),
            dma((2,)), dma((2,)),
        ],
        compiler_params=pltpu.CompilerParams(
            collective_id=0, has_side_effects=True, vmem_limit_bytes=49 * 2**20
        ),
    )(queries, key_rows, values, out_weight, out_grad)
    return store(*results)


def solution(mesh):
    blocks, cores = mesh.shape["seq"], mesh.shape["head"]

    def step(queries, key_rows, values, out_weight, out_grad):
        heads = queries.shape[1] // HEAD_DIM
        fits = cores == 2 and blocks == PLANE * PLANE and heads == blocks and out_weight.shape[1] % HEAD_DIM == 0
        fits = fits and out_weight.shape[0] == queries.shape[1] and out_weight.shape[0] % out_weight.shape[1] == 0
        if fits and out_weight.shape[1] * blocks == queries.shape[1] * cores:
            return fused(blocks, queries, key_rows, values, out_weight, out_grad)
        return per_device(queries, key_rows, values, out_weight, out_grad)

    placed = (
        P("seq", "head"),
        P("seq", "head"),
        P("seq", "head"),
        P("head", "seq"),
        P("seq", "head"),
    )
    return jax.shard_map(
        step,
        mesh=mesh,
        in_specs=placed,
        out_specs=(P("seq", "head"), P("seq", "head"), P("seq", "head"), P("seq", "head")),
        check_vma=False,
    )
```

profile of v0, /device:TPU:0, one launch (start us, length us, event | category | flops | bytes accessed | tf_op | source)
XLA Modules:
  0.0 169.9 jit_solution(16912747114811568568)
XLA Ops:
  0.6 167.2 %shard_map.84 = (bf16[256,2048]{1,0:T(8,128)(2,1)S(1)}, bf16[256,2048]{1,0:T(8,128)(2,1)S(1)}, bf16[256,2048]{1,0:T(8,128)(2,1)S(1)}, bf16[256,2048]{1,0:T(8,128)(2,1)S(1)}) custom-call(bf16[256,2048]{1,0:T(8,128)(2,1)} %q_in.1, bf16[256,2048]{1,0:T(8,128)(2,1)} %k_in.1, bf16[256,2048]{1,0:T(8,128)(2,1)} %v_in.1, bf16[2048,256]{1,0:T(8,128)(2,1)} %w_ref.1, ...), custom_call_target="tpu_custom_call" | custom-call | tf_op jit(solution)/shard_map/pallas_call | solution.py:600
  167.8 2.0 %shard_map.85 = (bf16[256,2048]{1,0:T(8,128)(2,1)}, bf16[256,2048]{1,0:T(8,128)(2,1)}, bf16[256,2048]{1,0:T(8,128)(2,1)}, bf16[256,2048]{1,0:T(8,128)(2,1)}) custom-call(bf16[256,2048]{1,0:T(8,128)(2,1)S(1)} %get-tuple-element.8.refs_0_, bf16[256,2048]{1,0:T(8,128)(2,1)S(1)} %get-tuple-element.9.refs_1_, bf16[256,2048]{1,0:T(8,128)(2,1)S(1)} %get-tuple-element.10.refs_2_, ...), custom_call_target="tpu_custom_call" | custom-call | tf_op jit(solution)/shard_map/pallas_call | solution.py:573
where the time goes:
time: 171 us; the launch traced here: 170 us
  Pallas kernels  169 us (99%)
    pallas_call x1, Pallas kernels, fused(): pl.pallas_call(functools.partial(kernel, blocks), out_shape=(out, out, ou...  167 us

commit v1 on v0

--- a/solution.py
+++ b/solution.py
@@ -10,6 +10,7 @@
 HEAD_DIM = 128
 MESH = pl.DeviceIdType.MESH
 PLANE = 4
+CHUNKS = 8
 
 
 def prefix_2(value, axis, combine, identity):
@@ -125,58 +126,61 @@
     )
 
 
-def visit_tables(planes):
-    half, rows = planes // 2, []
-    for own in range(planes):
-        rows.append(sorted(range(planes), key=lambda other: (other // half != own // half, abs(other - own))))
-    return rows
-
-
-def pick(table, position):
-    found = jnp.int32(table[0])
-    for at in range(1, len(table)):
-        found = jnp.where(position == at, jnp.int32(table[at]), found)
-    return found
-
-
 def kernel(
-    blocks, q_in, k_in, v_in, w_ref, g_ref,
+    blocks, chunks, q_in, k_in, v_in, w_ref, g_ref,
     mixed_ref, dq_ref, dk_ref, dv_ref,
     q_ref, k_ref, v_ref, w_all, g_all, st_send, st_recv, pre_send, prefix, lg_send, lg_recv, suf_send, suffix,
-    out_dir, normed, inv_spread, weights, attended, p_own, p_send, p_recv, ng, k_part, v_part,
-    x_send, x_recv,
-    w_recv_sem, wx_sem, wy_sem, wz_sem, local_sem, g_sem, a_send_sem, a_recv_sem, p_send_sem, p_recv_sem,
+    out_dir, od_send, od_recv, normed, inv_spread, weights, att, p_own, p_send, p_recv, m_send, m_recv,
+    ng, k_part, v_part, x_send, x_recv,
+    w_recv_sem, wy_sem, wi_sem, wo_sem, local_sem, g_send_sem, g_recv_sem, a_send_sem, a_recv_sem,
+    p_send_sem, p_recv_sem, m_send_sem, m_recv_sem, t_send_sem, t_recv_sem, o_send_sem, o_recv_sem,
     x_send_sem, x_recv_sem,
 ):
     me = lax.axis_index("seq")
     core = lax.axis_index("head")
     other = 1 - core
     planes = blocks // PLANE
-    half_planes = planes // 2
     size = blocks // 2
     share = st_send.shape[0] // size
     team, rank = me // size, lax.rem(me, size)
     spot = lax.rem(me, PLANE)
     level = me // PLANE
     bit_x, bit_y = lax.rem(spot, 2), spot // 2
-    spot_x = spot + 1 - 2 * bit_x
-    spot_y = spot + 2 - 4 * bit_y
-    spot_d = spot_x + 2 - 4 * bit_y
     length, width = q_ref.shape
     heads = width // HEAD_DIM
     rows, cols = w_ref.shape
-    half = rows // 2
-    per_core = blocks // 2
+    chunk = rows // chunks
+    per = chunks // 2
+    chunk_heads = chunk // HEAD_DIM
+    lower = level < planes // 2
+    middle = jnp.where(lower, level, planes - 1 - level) > 0
+    edge = jnp.logical_not(middle)
+    nbr_x = me + 1 - 2 * bit_x
+    nbr_y = me + 2 - 4 * bit_y
+    step_in = jnp.where(lower, PLANE, -PLANE)
+    inner = me + step_in
+    outer = jnp.where(middle, me - step_in, inner)
 
     def at_seq(position):
         return (position, core)
 
-    nbr_x = level * PLANE + spot_x
-    nbr_y = level * PLANE + spot_y
-
-    q_load = pltpu.make_async_copy(q_in, q_ref, local_sem.at[2])
-    k_load = pltpu.make_async_copy(k_in, k_ref, local_sem.at[3])
-    v_load = pltpu.make_async_copy(v_in, v_ref, local_sem.at[4])
+    def own_col(k):
+        return jnp.where(lower, k, planes - 1 - k) * 2 + bit_y
+
+    def other_col(k):
+        return jnp.where(lower, k, planes - 1 - k) * 2 + 1 - bit_y
+
+    o0, o1, o2, o3 = (own_col(k) for k in range(4))
+    c0, c1, c2, c3 = (other_col(k) for k in range(4))
+    mine = me // 2
+    near_own = jnp.where(middle, o0, o1)
+    near_other, next_other = jnp.where(middle, c1, c0), jnp.where(middle, c0, c1)
+    groups = ((mine, near_own, near_other), (o2, next_other), (o3, c2), (c3,))
+
+    q_load = pltpu.make_async_copy(q_in, q_ref, local_sem.at[0])
+    k_load = pltpu.make_async_copy(k_in, k_ref, local_sem.at[1])
+    v_load = pltpu.make_async_copy(v_in, v_ref, local_sem.at[2])
+    own_w = pltpu.make_async_copy(w_ref, w_all.at[mine], local_sem.at[3])
     k_load.start()
     v_load.start()
     barrier = pltpu.get_barrier_semaphore()
@@ -188,11 +192,44 @@
     lax.fori_loop(1, blocks, greet, 0)
     pl.semaphore_signal(barrier, inc=1, device_id=(me, other), device_id_type=MESH)
 
-    own_w = pltpu.make_async_copy(w_ref, w_all.at[me], local_sem.at[0])
-    own_g = pltpu.make_async_copy(g_ref, g_all.at[core], local_sem.at[1])
+    half = size // 2
+    own_rows, far_rows = pl.ds(0, length), pl.ds(length, length)
+
+    def grad_cols(j, parity):
+        return pl.ds(pl.multiple_of((lax.rem(j, half) * 2 + parity) * cols, cols), cols)
+
+    def own_grad(i):
+        j = core * half + i
+        return pltpu.make_async_copy(g_ref.at[:, grad_cols(j, bit_x)], g_all.at[j, own_rows], local_sem.at[4 + i])
+
+    def grad_core(i):
+        j = core * half + i
+        return pltpu.make_async_remote_copy(
+            src_ref=g_ref.at[:, grad_cols(j, bit_x)], dst_ref=g_all.at[j, own_rows],
+            send_sem=g_send_sem.at[0, i], recv_sem=g_recv_sem.at[0, i],
+            device_id=(me, other), device_id_type=MESH,
+        )
+
+    def grad_pair(i):
+        j = core * half + i
+        return pltpu.make_async_remote_copy(
+            src_ref=g_ref.at[:, grad_cols(j, 1 - bit_x)], dst_ref=g_all.at[j, far_rows],
+            send_sem=g_send_sem.at[1, i], recv_sem=g_recv_sem.at[1, i],
+            device_id=at_seq(nbr_x), device_id_type=MESH,
+        )
+
+    def grad_relay(i):
+        j = core * half + i
+        return pltpu.make_async_remote_copy(
+            src_ref=g_all.at[j, far_rows], dst_ref=g_all.at[j, far_rows],
+            send_sem=g_send_sem.at[2, i], recv_sem=g_recv_sem.at[2, i],
+            device_id=(me, other), device_id_type=MESH,
+        )
+
     q_load.start()
     own_w.start()
-    own_g.start()
+    for i in range(half):
+        own_grad(i).start()
     k_load.wait()
     v_load.wait()
 
@@ -275,108 +312,110 @@
         def _():
             team_total(kind).start()
 
-    g_copy = pltpu.make_async_remote_copy(
-        src_ref=g_ref, dst_ref=g_all.at[core], send_sem=g_sem.at[0], recv_sem=g_sem.at[1],
-        device_id=(me, other), device_id_type=MESH,
-    )
-    g_copy.start()
-    exchange(pair_of(st_send), slot_of(st_recv), 0, True)
-
-    def piece(block, part, sems, target, own=False):
-        span = pl.ds(part * half, half)
-        return pltpu.make_async_remote_copy(
-            src_ref=w_ref.at[span] if own else w_all.at[block, span],
-            dst_ref=w_all.at[block, span],
-            send_sem=sems.at[block, part], recv_sem=w_recv_sem.at[block, part],
+    def span_of(c):
+        return pl.ds(pl.multiple_of(c * chunk, chunk), chunk)
+
+    def piece(j, c, sems, target, own=False):
+        span = span_of(c)
+        return pltpu.make_async_remote_copy(
+            src_ref=w_ref.at[span] if own else w_all.at[j, span],
+            dst_ref=w_all.at[j, span],
+            send_sem=sems.at[j, c], recv_sem=w_recv_sem.at[j, c],
             device_id=at_seq(target), device_id_type=MESH,
         )
 
-    up_ok = level + 1 < planes
-    down_ok = level > 0
-    up = jnp.minimum(me + PLANE, blocks - PLANE + spot)
-    down = jnp.maximum(me - PLANE, spot)
-
-    for part in range(2):
-        piece(me, part, wx_sem, nbr_x, True).start()
-        piece(me, part, wy_sem, nbr_y, True).start()
-
-        @pl.when(up_ok)
+    def to_y(j, c, own=False):
+        return piece(j, c, wy_sem, nbr_y, own)
+
+    def to_inner(j, c, own=False):
+        return piece(j, c, wi_sem, inner, own)
+
+    def to_outer(j, c, own=False):
+        return piece(j, c, wo_sem, outer, own)
+
+    def landed(j, c):
+        to_y(j, c).wait_recv()
+
+    def own_piece(c, finish=False):
+        for copy in (to_y(mine, c, True), to_inner(mine, c, True)):
+            copy.wait_send() if finish else copy.start()
+
+        @pl.when(middle)
         def _():
-            piece(me, part, wz_sem.at[0], up, True).start()
-
-        @pl.when(down_ok)
-        def _():
-            piece(me, part, wz_sem.at[1], down, True).start()
-
-    tables = visit_tables(planes)
-    order = [pick([tables[z][k] for z in range(planes)], level) for k in range(planes)]
-
-    def passing(k):
-        return jnp.where(order[k] < level, up_ok, down_ok)
-
-    def along_z(k, where, finish=False):
-        plane = order[k]
-        block = plane * PLANE + where
-        going_up = plane < level
-        for part in range(2):
-            for sems, way, go in ((wz_sem.at[0], up, going_up), (wz_sem.at[1], down, jnp.logical_not(going_up))):
-
-                @pl.when(jnp.logical_and(go, passing(k)))
+            copy = to_outer(mine, c, True)
+            copy.wait_send() if finish else copy.start()
+
+    def routed(c):
+        return lax.rem(c, 2) == 1
+
+    def pump(phase, c, finish=False):
+        def move(j, ways):
+            if not finish:
+                landed(j, c)
+            for way in ways:
+                copy = way(j, c)
+                copy.wait_send() if finish else copy.start()
+
+        if phase == 0:
+
+            @pl.when(edge)
+            def _():
+                move(c0, (to_inner,))
+                move(o1, (to_y,))
+
+            @pl.when(middle)
+            def _():
+                move(o0, (to_inner,))
+                move(o2, (to_outer, to_y))
+
+        elif phase == 1:
+
+            @pl.when(edge)
+            def _():
+                move(o2, (to_y,))
+
+            @pl.when(middle)
+            def _():
+                move(o3, (to_outer, to_y))
+
+        else:
+
+            @pl.when(edge)
+            def _():
+                if not finish:
+                    landed(o3, c)
+
+                @pl.when(jnp.logical_not(routed(c)))
                 def _():
-                    copy = piece(block, part, sems, way)
-                    if finish:
-                        copy.wait_send()
-                    else:
-                        copy.wait_recv()
-                        copy.start()
-
-    def end_of_z(k, where, part):
-        @pl.when(jnp.logical_not(passing(k)))
-        def _():
-            piece(order[k] * PLANE + where, part, wx_sem, nbr_x).wait_recv()
-
-    def across(k, finish=False):
-        block = order[k] * PLANE + spot
-        for part in range(2):
-            if not finish:
-                end_of_z(k, spot, part)
-            for copy in (piece(block, part, wx_sem, nbr_x), piece(block, part, wy_sem, nbr_y)):
-                copy.wait_send() if finish else copy.start()
-
-    def relay_step(k, finish=False):
-        plane = order[k]
-        to_x = piece(plane * PLANE + spot_y, 0, wx_sem, nbr_x)
-        to_y = piece(plane * PLANE + spot_x, 1, wy_sem, nbr_y)
-        for copy in (to_x, to_y):
-            if finish:
-                copy.wait_send()
-            else:
-                copy.wait_recv()
-                copy.start()
-
-    def cross_step(k, finish=False):
-        block = order[k] * PLANE + spot_d
-        for part in range(2):
-
-            @pl.when(level == half_planes - 1)
+                    copy = to_y(o3, c)
+                    copy.wait_send() if finish else copy.start()
+
+            @pl.when(middle)
             def _():
-                copy = piece(block, part, wz_sem.at[0], up)
-                copy.wait_send() if finish else copy.start()
-
-            @pl.when(level == half_planes)
+                if not finish:
+                    landed(c3, c)
+
+                @pl.when(routed(c))
+                def _():
+                    copy = to_outer(c3, c)
+                    copy.wait_send() if finish else copy.start()
+
+    def settle(group, c):
+        if group == 0:
+
+            @pl.when(middle)
             def _():
-                copy = piece(block, part, wz_sem.at[1], down)
-                copy.wait_send() if finish else copy.start()
-
-    def settle(k):
-        plane = order[k]
-        near = ((spot_y, 1), (spot_x, 0), (spot_d, 0), (spot_d, 1))
-        far = ((spot_y, 0), (spot_x, 0), (spot_y, 1), (spot_x, 1))
-        for where, part in near if k < half_planes else far:
-            piece(plane * PLANE + where, part, wx_sem, nbr_x).wait_recv()
-        if k >= half_planes:
-            for part in range(2):
-                end_of_z(k, spot_d, part)
+                landed(c1, c)
+
+        elif group == 1:
+            landed(next_other, c)
+        elif group == 2:
+            landed(c2, c)
+        else:
+
+            @pl.when(edge)
+            def _():
+                landed(c3, c)
 
     causal = lower_mask(length)
 
@@ -394,29 +433,40 @@
         value = numerator * inv
         normed[h] = value
         inv_spread[h] = jnp.broadcast_to(inv, (length, HEAD_DIM))
-        attended[:, c] = value.astype(jnp.bfloat16)
-        return carry
-
-    tile = cols
-    n_tiles = rows // tile
-
-    def grad_cols(block):
-        return g_all[block // per_core, :, pl.ds(pl.multiple_of(lax.rem(block, per_core) * cols, cols), cols)]
-
-    def direction_step(k):
-        base = order[k] * PLANE
-
-        def one(n, carry):
-            span = pl.ds(pl.multiple_of(n * tile, tile), tile)
-            total = contract_cols(grad_cols(base), w_all[base, span])
-            for s in range(1, PLANE):
-                total = total + contract_cols(grad_cols(base + s), w_all[base + s, span])
-            if k > 0:
-                total = total + out_dir[:, span]
+        att[own_rows, c] = value.astype(jnp.bfloat16)
+        return carry
+
+    quarter = width // 4
+
+    def att_copy(i):
+        c = pl.ds(i * quarter, quarter)
+        return pltpu.make_async_remote_copy(
+            src_ref=att.at[own_rows, c], dst_ref=att.at[far_rows, c],
+            send_sem=t_send_sem.at[i], recv_sem=t_recv_sem.at[i],
+            device_id=at_seq(nbr_x), device_id_type=MESH,
+        )
+
+    def od_copy(c):
+        return pltpu.make_async_remote_copy(
+            src_ref=od_send.at[c], dst_ref=od_recv.at[c],
+            send_sem=o_send_sem.at[c], recv_sem=o_recv_sem.at[c],
+            device_id=at_seq(nbr_x), device_id_type=MESH,
+        )
+
+    def direction_step(group, c):
+        span = span_of(c)
+        total = None
+        for j in groups[group]:
+            term = contract_cols(g_all[j], w_all[j, span])
+            total = term if total is None else total + term
+        if group > 0:
+            total = total + out_dir[:, span]
+        if group < len(groups) - 1:
             out_dir[:, span] = total
-            return carry
-
-        lax.fori_loop(0, n_tiles, one, 0)
+        else:
+            out_dir[own_rows, span] = total[:length]
+            od_send[c] = total[length:].astype(jnp.bfloat16)
+            od_copy(c).start()
 
     def p_copy(slot):
         return pltpu.make_async_remote_copy(
@@ -425,80 +475,52 @@
             device_id=(me, other), device_id_type=MESH,
         )
 
-    def partial_step(k):
-        def one(s, carry):
-            block = order[k] * PLANE + s
-            term = contract_mid(attended[...], w_all[block]).astype(jnp.bfloat16)
-            slot = lax.rem(block, per_core)
-
-            @pl.when(block // per_core == core)
-            def _():
-                p_own[slot] = term
-
-            @pl.when(block // per_core != core)
-            def _():
-                p_send[slot] = term
-                p_copy(slot).start()
-
-            return carry
-
-        lax.fori_loop(0, PLANE, one, 0)
-
-    q_load.wait()
-    lax.fori_loop(0, heads, score_step, 0)
-    relay_step(0)
-    along_z(1, spot)
-    across(1)
-    along_z(2, spot)
-    arrived(pair_of(st_send), slot_of(st_recv), 0)
-    running(0, 0, st_recv, pre_send, prefix, False)
-    exchange(slot_of(pre_send), pair_of(prefix), 1, True)
-    settle(0)
-    cross_step(0)
-    along_z(3, spot)
-    relay_step(1)
-    across(2)
-    own_w.wait()
-    own_g.wait()
-    g_copy.wait()
-    direction_step(0)
-    along_z(2, spot_d)
-    settle(1)
-    cross_step(1)
-    across(3)
-    direction_step(1)
-    arrived(slot_of(pre_send), pair_of(prefix), 1)
-    lax.fori_loop(0, heads, norm_step, 0)
-    partial_step(0)
-    along_z(3, spot_d)
-    partial_step(1)
-    settle(2)
-    direction_step(2)
-    partial_step(2)
-    settle(3)
-    direction_step(3)
+    def m_copy(slot):
+        return pltpu.make_async_remote_copy(
+            src_ref=m_send.at[slot], dst_ref=m_recv.at[slot],
+            send_sem=m_send_sem.at[slot], recv_sem=m_recv_sem.at[slot],
+            device_id=at_seq(nbr_x), device_id_type=MESH,
+        )
+
+    def partial_step(j):
+        term = contract_mid(att[...], w_all[j]).astype(jnp.bfloat16)
+        slot = lax.rem(j, half)
+
+        @pl.when(j // half == core)
+        def _():
+            p_own[slot] = term
+
+        @pl.when(j // half != core)
+        def _():
+            p_send[slot] = term
+            p_copy(slot).start()
+
+    def mixed_cols(slot, parity):
+        return pl.ds(pl.multiple_of((slot * 2 + parity) * cols, cols), cols)
+
+    def mix_step(slot, carry):
+        p_copy(slot).wait_recv()
+        both = (p_own[slot].astype(jnp.float32) + p_recv[slot].astype(jnp.float32)).astype(jnp.bfloat16)
+        m_send[slot] = both[length:]
+        m_copy(slot).start()
+        mixed_ref[:, mixed_cols(slot, bit_x)] = both[:length]
+        return carry
 
     def numer_step(h, carry):
         c = head_cols(h)
-        toward, unit = out_dir[:, c], normed[h]
+        sub = pl.ds(pl.multiple_of(lax.rem(h, chunk_heads) * HEAD_DIM, HEAD_DIM), HEAD_DIM)
+        toward = out_dir[own_rows, c] + od_recv[h // chunk_heads, :, sub].astype(jnp.float32)
+        unit = normed[h]
         along = jnp.mean(toward * unit, axis=-1, keepdims=True)
         low = ((toward - unit * along) * inv_spread[h]).astype(jnp.bfloat16)
         ng[:, c] = low
         lg_send[h] = contract_rows(q_ref[:, c], low).astype(jnp.bfloat16)
-
-        @pl.when(jnp.logical_and(h > 0, lax.rem(h, share) == 0))
-        def _():
-            leave(pair_of(lg_send), slot_of(lg_recv), 2, h // share - 1)
-
-        return carry
-
-    lax.fori_loop(0, heads, numer_step, 0)
-    leave(pair_of(lg_send), slot_of(lg_recv), 2, size - 1)
-    lg_recv[rank] = lg_send[pl.ds(rank * share, share)]
-    partial_step(planes - 1)
-    arrived(pair_of(lg_send), slot_of(lg_recv), 2)
-    running(1, 1, lg_recv, suf_send, suffix, True)
-    exchange(slot_of(suf_send), pair_of(suffix), 3, True)
+        return carry
+
+    def numer_chunk(c):
+        od_copy(c).wait_recv()
+        lax.fori_loop(c * chunk_heads, (c + 1) * chunk_heads, numer_step, 0)
+        leave(pair_of(lg_send), slot_of(lg_recv), 2, c)
 
     def pair_step(h, carry):
         c = head_cols(h)
@@ -509,15 +531,124 @@
         v_part[h] = contract_rows(weights[h], low)
         return carry
 
-    lax.fori_loop(0, heads, pair_step, 0)
-
-    def mix_step(slot, carry):
-        p_copy(slot).wait()
-        c = pl.ds(pl.multiple_of(slot * cols, cols), cols)
-        mixed_ref[:, c] = (p_own[slot].astype(jnp.float32) + p_recv[slot].astype(jnp.float32)).astype(jnp.bfloat16)
-        return carry
-
-    lax.fori_loop(0, per_core, mix_step, 0)
+    def each(count, body):
+        def one(i, carry):
+            body(i)
+            return carry
+
+        lax.fori_loop(0, count, one, 0)
+
+    exchange(pair_of(st_send), slot_of(st_recv), 0, True)
+    for i in range(half):
+        grad_core(i).start()
+        grad_pair(i).start()
+    each(per, own_piece)
+
+    q_load.wait()
+
+    def stage(i):
+        lax.fori_loop(i * (heads // per), (i + 1) * (heads // per), score_step, 0)
+        pump(0, i)
+
+    each(per, stage)
+    arrived(pair_of(st_send), slot_of(st_recv), 0)
+    running(0, 0, st_recv, pre_send, prefix, False)
+    exchange(slot_of(pre_send), pair_of(prefix), 1, True)
+    for i in range(half):
+        grad_pair(i).wait_recv()
+        grad_relay(i).start()
+    own_w.wait()
+    for i in range(half):
+        own_grad(i).wait()
+        grad_core(i).wait_recv()
+    each(per, lambda i: pump(1, i))
+    for i in range(half):
+        grad_relay(i).wait_recv()
+
+    def stage(i):
+        settle(0, i)
+        direction_step(0, i)
+
+    each(per, stage)
+    arrived(slot_of(pre_send), pair_of(prefix), 1)
+
+    def stage(i):
+        lax.fori_loop(i * (heads // per), (i + 1) * (heads // per), norm_step, 0)
+        att_copy(i).start()
+        pump(2, i)
+        settle(1, i)
+        direction_step(1, i)
+
+    for i in range(per):
+        stage(i)
+    each(per, lambda i: own_piece(per + i))
+
+    def stage(i):
+        settle(2, i)
+        direction_step(2, i)
+
+    each(per, stage)
+
+    def stage(i):
+        settle(3, i)
+        direction_step(3, i)
+
+    each(per, stage)
+
+    def stage(i):
+        pump(0, per + i)
+        numer_chunk(i)
+
+    each(per, stage)
+    for i in range(4):
+        att_copy(i).wait_recv()
+
+    def stage(i):
+        pump(1, per + i)
+        settle(0, per + i)
+        direction_step(0, per + i)
+        lax.fori_loop(i * chunk_heads, (i + 1) * chunk_heads, pair_step, 0)
+
+    each(per, stage)
+    for j in groups[0]:
+        partial_step(j)
+
+    def stage(i):
+        pump(2, per + i)
+        settle(1, per + i)
+        direction_step(1, per + i)
+
+    each(per, stage)
+    for j in groups[1]:
+        partial_step(j)
+
+    def stage(i):
+        settle(2, per + i)
+        direction_step(2, per + i)
+
+    each(per, stage)
+
+    def stage(i):
+        settle(3, per + i)
+        direction_step(3, per + i)
+
+    each(per, stage)
+    for j in groups[2] + groups[3]:
+        partial_step(j)
+    each(per, lambda i: numer_chunk(per + i))
+    lg_recv[rank] = lg_send[pl.ds(rank * share, share)]
+    lax.fori_loop(0, half, mix_step, 0)
+    arrived(pair_of(lg_send), slot_of(lg_recv), 2)
+    running(1, 1, lg_recv, suf_send, suffix, True)
+    exchange(slot_of(suf_send), pair_of(suffix), 3, True)
+    lax.fori_loop(heads // 2, heads, pair_step, 0)
+
+    def take_mixed(slot, carry):
+        m_copy(slot).wait_recv()
+        mixed_ref[:, mixed_cols(slot, 1 - bit_x)] = m_recv[slot]
+        return carry
+
+    lax.fori_loop(0, half, take_mixed, 0)
     arrived(slot_of(suf_send), pair_of(suffix), 3)
 
     def last_step(h, carry):
@@ -528,26 +659,21 @@
 
     lax.fori_loop(0, heads, last_step, 0)
 
-    for part in range(2):
-        piece(me, part, wx_sem, nbr_x, True).wait_send()
-        piece(me, part, wy_sem, nbr_y, True).wait_send()
-
-        @pl.when(up_ok)
-        def _():
-            piece(me, part, wz_sem.at[0], up, True).wait_send()
-
-        @pl.when(down_ok)
-        def _():
-            piece(me, part, wz_sem.at[1], down, True).wait_send()
-
-    for k in range(1, planes):
-        along_z(k, spot, True)
-        across(k, True)
-    for k in range(half_planes):
-        relay_step(k, True)
-        cross_step(k, True)
-    for k in range(half_planes, planes):
-        along_z(k, spot_d, True)
+    def finish(c):
+        own_piece(c, True)
+        for phase in range(3):
+            pump(phase, c, True)
+        od_copy(c).wait_send()
+
+    each(chunks, finish)
+
+    def finish(i):
+        for copy in (grad_core(i), grad_pair(i), grad_relay(i), p_copy(i), m_copy(i)):
+            copy.wait_send()
+
+    each(half, finish)
+    for i in range(4):
+        att_copy(i).wait_send()
     exchange(pair_of(st_send), slot_of(st_recv), 0, False)
     exchange(slot_of(pre_send), pair_of(prefix), 1, False)
     exchange(pair_of(lg_send), slot_of(lg_recv), 2, False)
@@ -584,40 +710,49 @@
     length, width = queries.shape
     heads = width // HEAD_DIM
     rows, cols = out_weight.shape
-    per_core = blocks // 2
     low, wide = jnp.bfloat16, jnp.float32
     size = blocks // 2
+    half = size // 2
     share = heads // size
+    chunks = CHUNKS
     state = pltpu.VMEM((heads, HEAD_DIM, HEAD_DIM), low)
     slots = pltpu.VMEM((size, share, HEAD_DIM, HEAD_DIM), low)
     totals = pltpu.VMEM((2, share, HEAD_DIM, HEAD_DIM), wide)
     by_head = pltpu.VMEM((heads, length, HEAD_DIM), wide)
     flat = pltpu.VMEM((length, width), low)
-    parts = pltpu.VMEM((per_core, length, cols), low)
+    parts = pltpu.VMEM((half, 2 * length, cols), low)
+    shares = pltpu.VMEM((half, length, cols), low)
+    steps = pltpu.VMEM((chunks, length, rows // chunks), low)
     dma = pltpu.SemaphoreType.DMA
     out = jax.ShapeDtypeStruct((length, width), low)
     vmem, in_hbm = pl.BlockSpec(memory_space=pltpu.VMEM), pl.BlockSpec(memory_space=pltpu.HBM)
+    pieces = dma((size, chunks))
     results = pl.pallas_call(
-        functools.partial(kernel, blocks),
+        functools.partial(kernel, blocks, chunks),
         out_shape=(out, out, out, out),
         in_specs=[in_hbm] * 5,
         out_specs=(vmem, vmem, vmem, vmem),
         scratch_shapes=[
             flat, flat, flat,
-            pltpu.VMEM((blocks, rows, cols), low),
-            pltpu.VMEM((2, length, width), low),
+            pltpu.VMEM((size, rows, cols), low),
+            pltpu.VMEM((size, 2 * length, cols), low),
             state, slots, slots, state, state, slots, slots, state,
-            pltpu.VMEM((length, rows), wide),
+            pltpu.VMEM((2 * length, rows), wide),
+            steps, steps,
             by_head, by_head,
             pltpu.VMEM((heads, length, length), low),
-            flat, parts, parts, parts, flat, by_head, by_head,
+            pltpu.VMEM((2 * length, width), low),
+            parts, parts, parts, shares, shares,
+            flat, by_head, by_head,
             totals, totals,
-            dma((blocks, 2)), dma((blocks, 2)), dma((blocks, 2)), dma((2, blocks, 2)),
-            dma((5,)), dma((2,)), dma((4, blocks)), dma((4, blocks)), dma((per_core,)), dma((per_core,)),
+            pieces, pieces, pieces, pieces,
+            dma((4 + half,)), dma((3, half)), dma((3, half)), dma((4, blocks)), dma((4, blocks)),
+            dma((half,)), dma((half,)), dma((half,)), dma((half,)), dma((4,)), dma((4,)),
+            dma((chunks,)), dma((chunks,)),
             dma((2,)), dma((2,)),
         ],
         compiler_params=pltpu.CompilerParams(
-            collective_id=0, has_side_effects=True, vmem_limit_bytes=49 * 2**20
+            collective_id=0, has_side_effects=True, vmem_limit_bytes=44 * 2**20
         ),
     )(queries, key_rows, values, out_weight, out_grad)
     return store(*results)

time: 171 us -> 152 us (0.89)
  Pallas kernels: 169 us -> 145 us
  local copies, waits for them, and re-layouts: 0 us -> 6.11 us
    pallas_call x1, Pallas kernels: 167 us -> 143 us  [fused(): pl.pallas_call(functools.partial(kernel, blocks, chunks), out_shape=(out,...]
    unnamed x0 -> x10, local copies, waits for them, and re-layouts: none -> 6.11 us
where the time goes in v1:
time: 152 us; the launch traced here: 151 us
  Pallas kernels  145 us (95%)
  local copies, waits for them, and re-layouts  6.11 us (4%)
    pallas_call x1, Pallas kernels, fused(): pl.pallas_call(functools.partial(kernel, blocks, chunks), out_shape=(out,...  143 us
    unnamed x10, local copies, waits for them, and re-layouts  6.11 us

profile of v1, /device:TPU:0, one launch (start us, length us, event | category | flops | bytes accessed | tf_op | source)
XLA Modules:
  0.0 151.3 jit_solution(11078226000262362712)
XLA Ops:
  0.6 0.0 copy-start
  0.6 1.2 copy-done
  1.9 0.0 copy-start.1
  1.9 1.2 copy-done.1
  3.1 0.0 copy-start.2
  3.1 1.2 copy-done.2
  4.3 0.0 copy-start.3
  4.3 1.2 copy-done.3
  5.5 0.0 copy-start.4
  5.5 1.2 copy-done.4
  6.8 142.5 %shard_map.84 = (bf16[256,2048]{1,0:T(8,128)(2,1)S(1)}, bf16[256,2048]{1,0:T(8,128)(2,1)S(1)}, bf16[256,2048]{1,0:T(8,128)(2,1)S(1)}, bf16[256,2048]{1,0:T(8,128)(2,1)S(1)}) custom-call(bf16[256,2048]{1,0:T(8,128)(2,1)S(1)} %copy-done, bf16[256,2048]{1,0:T(8,128)(2,1)S(1)} %copy-done.1, bf16[256,2048]{1,0:T(8,128)(2,1)S(1)} %copy-done.2, ...), custom_call_target="tpu_custom_call" | custom-call | tf_op jit(solution)/shard_map/pallas_call | solution.py:730
  149.3 2.0 %shard_map.85 = (bf16[256,2048]{1,0:T(8,128)(2,1)}, bf16[256,2048]{1,0:T(8,128)(2,1)}, bf16[256,2048]{1,0:T(8,128)(2,1)}, bf16[256,2048]{1,0:T(8,128)(2,1)}) custom-call(bf16[256,2048]{1,0:T(8,128)(2,1)S(1)} %get-tuple-element.8.refs_0_, bf16[256,2048]{1,0:T(8,128)(2,1)S(1)} %get-tuple-element.9.refs_1_, bf16[256,2048]{1,0:T(8,128)(2,1)S(1)} %get-tuple-element.10.refs_2_, ...), custom_call_target="tpu_custom_call" | custom-call | tf_op jit(solution)/shard_map/pallas_call | solution.py:699
Async XLA Ops:
  0.6 1.2 copy-start
  1.9 1.2 copy-start.1
  3.1 1.2 copy-start.2
  4.3 1.2 copy-start.3
  5.5 1.2 copy-start.4

commit v2 on v1

--- a/solution.py
+++ b/solution.py
@@ -10,7 +10,8 @@
 HEAD_DIM = 128
 MESH = pl.DeviceIdType.MESH
 PLANE = 4
-CHUNKS = 8
+PARTS = (3, 3, 2)
+TILE = 64
 
 
 def prefix_2(value, axis, combine, identity):
@@ -127,22 +128,20 @@
 
 
 def kernel(
-    blocks, chunks, q_in, k_in, v_in, w_ref, g_ref,
+    blocks, chunks, parts, q_in, k_in, v_in, w_ref, g_ref,
     mixed_ref, dq_ref, dk_ref, dv_ref,
-    q_ref, k_ref, v_ref, w_all, g_all, st_send, st_recv, pre_send, prefix, lg_send, lg_recv, suf_send, suffix,
+    q_ref, k_ref, v_ref, w_all, g_all, st_send, prefix, lg_send, suffix, a_buf, b_send, b_buf, c_send,
     out_dir, od_send, od_recv, normed, inv_spread, weights, att, p_own, p_send, p_recv, m_send, m_recv,
-    ng, k_part, v_part, x_send, x_recv,
-    w_recv_sem, wy_sem, wi_sem, wo_sem, local_sem, g_send_sem, g_recv_sem, a_send_sem, a_recv_sem,
+    ng, k_part, v_part,
+    w_recv_sem, wy_sem, wi_sem, wo_sem, local_sem, g_send_sem, g_recv_sem,
+    a_send_sem, a_recv_sem, b_send_sem, b_recv_sem, c_send_sem, c_recv_sem,
     p_send_sem, p_recv_sem, m_send_sem, m_recv_sem, t_send_sem, t_recv_sem, o_send_sem, o_recv_sem,
-    x_send_sem, x_recv_sem,
 ):
     me = lax.axis_index("seq")
     core = lax.axis_index("head")
     other = 1 - core
     planes = blocks // PLANE
     size = blocks // 2
-    share = st_send.shape[0] // size
-    team, rank = me // size, lax.rem(me, size)
     spot = lax.rem(me, PLANE)
     level = me // PLANE
     bit_x, bit_y = lax.rem(spot, 2), spot // 2
@@ -150,7 +149,6 @@
     heads = width // HEAD_DIM
     rows, cols = w_ref.shape
     chunk = rows // chunks
-    per = chunks // 2
     chunk_heads = chunk // HEAD_DIM
     lower = level < planes // 2
     middle = jnp.where(lower, level, planes - 1 - level) > 0
@@ -186,10 +184,11 @@
     barrier = pltpu.get_barrier_semaphore()
 
     def greet(i, carry):
-        pl.semaphore_signal(barrier, inc=1, device_id=at_seq(lax.rem(me + i, blocks)), device_id_type=MESH)
+        for mate in (level * PLANE + lax.rem(spot + i, PLANE), lax.rem(level + i, planes) * PLANE + spot):
+            pl.semaphore_signal(barrier, inc=1, device_id=at_seq(mate), device_id_type=MESH)
         return carry
 
-    lax.fori_loop(1, blocks, greet, 0)
+    lax.fori_loop(1, PLANE, greet, 0)
     pl.semaphore_signal(barrier, inc=1, device_id=(me, other), device_id_type=MESH)
 
     half = size // 2
@@ -230,87 +229,126 @@
     own_w.start()
     for i in range(half):
         own_grad(i).start()
-    k_load.wait()
-    v_load.wait()
-
     def head_cols(h):
         return pl.ds(pl.multiple_of(h * HEAD_DIM, HEAD_DIM), HEAD_DIM)
 
     def make_state(h, carry):
         c = head_cols(h)
-        st_send[h] = contract_rows(k_ref[:, c], v_ref[:, c]).astype(jnp.bfloat16)
+        st_send[c] = contract_rows(k_ref[:, c], v_ref[:, c]).astype(jnp.bfloat16)
         return carry
 
-    lax.fori_loop(0, heads, make_state, 0)
-    st_recv[rank] = st_send[pl.ds(rank * share, share)]
-
-    pl.semaphore_wait(barrier, blocks)
-
-    def state_copy(src, dst, kind, peer):
-        return pltpu.make_async_remote_copy(
-            src_ref=src(peer), dst_ref=dst(rank),
-            send_sem=a_send_sem.at[kind, peer], recv_sem=a_recv_sem.at[kind, rank],
-            device_id=at_seq(team * size + peer), device_id_type=MESH,
-        )
-
-    def leave(src, dst, kind, peer):
-        @pl.when(peer != rank)
-        def _():
-            state_copy(src, dst, kind, peer).start()
-
-    def exchange(src, dst, kind, start):
+    def at_of(kind):
+        first, count = (0, chunks) if kind == 0 else (sum(parts[: kind - 1]), parts[kind - 1])
+        quarter = count * chunk // PLANE
+        return first * chunk, first * chunk // PLANE, quarter
+
+    def a_copy(kind, peer, sender):
+        base, packed, quarter = at_of(kind)
+        source = st_send if kind == 0 else lg_send
+        return pltpu.make_async_remote_copy(
+            src_ref=source.at[pl.ds(base + peer * quarter, quarter)],
+            dst_ref=a_buf.at[min(kind, 1), sender, pl.ds(packed, quarter)],
+            send_sem=a_send_sem.at[kind, peer], recv_sem=a_recv_sem.at[kind, sender],
+            device_id=at_seq(level * PLANE + peer), device_id_type=MESH,
+        )
+
+    def b_copy(kind, plane, sender):
+        packed, quarter = at_of(kind)[1:]
+        return pltpu.make_async_remote_copy(
+            src_ref=b_send.at[min(kind, 1), pl.ds(packed, quarter)],
+            dst_ref=b_buf.at[min(kind, 1), sender, pl.ds(packed, quarter)],
+            send_sem=b_send_sem.at[kind, plane], recv_sem=b_recv_sem.at[kind, sender],
+            device_id=at_seq(plane * PLANE + spot), device_id_type=MESH,
+        )
+
+    def c_copy(kind, peer, sender):
+        base, packed, quarter = at_of(kind)
+        target = prefix if kind == 0 else suffix
+        return pltpu.make_async_remote_copy(
+            src_ref=c_send.at[min(kind, 1), peer, pl.ds(packed, quarter)],
+            dst_ref=target.at[pl.ds(base + sender * quarter, quarter)],
+            send_sem=c_send_sem.at[kind, peer], recv_sem=c_recv_sem.at[kind, sender],
+            device_id=at_seq(level * PLANE + peer), device_id_type=MESH,
+        )
+
+    def mates(body):
         def one(i, carry):
-            copy = state_copy(src, dst, kind, lax.rem(rank + i, size))
-            copy.start() if start else copy.wait_send()
+            body(lax.rem(spot + i, PLANE))
             return carry
 
-        lax.fori_loop(1, size, one, 0)
-
-    def arrived(src, dst, kind):
+        lax.fori_loop(1, PLANE, one, 0)
+
+    def later(kind, body):
         def one(i, carry):
-            peer = lax.rem(rank + i, size)
-            pltpu.make_async_remote_copy(
-                src_ref=src(rank), dst_ref=dst(peer),
-                send_sem=a_send_sem.at[kind, rank], recv_sem=a_recv_sem.at[kind, peer],
-                device_id=at_seq(team * size + peer), device_id_type=MESH,
-            ).wait_recv()
+            plane = level + i if kind == 0 else level - i
+
+            @pl.when(jnp.logical_and(plane >= 0, plane < planes))
+            def _():
+                body(jnp.clip(plane, 0, planes - 1))
+
             return carry
 
-        lax.fori_loop(1, size, one, 0)
-
-    def pair_of(ref):
-        return lambda owner: ref.at[pl.ds(owner * share, share)]
-
-    def slot_of(ref):
-        return lambda owner: ref.at[owner]
-
-    def team_total(kind):
-        return pltpu.make_async_remote_copy(
-            src_ref=x_send.at[kind], dst_ref=x_recv.at[kind],
-            send_sem=x_send_sem.at[kind], recv_sem=x_recv_sem.at[kind],
-            device_id=at_seq((1 - team) * size + rank), device_id_type=MESH,
-        )
-
-    def running(first_team, kind, source, low_send, low_own, backwards):
-        @pl.when(team == first_team)
-        def _():
-            x_recv[kind] = jnp.zeros(x_recv.shape[1:], jnp.float32)
-
-        @pl.when(team != first_team)
-        def _():
-            team_total(kind).wait_recv()
-
-        def one(i, total):
-            at = size - 1 - i if backwards else i
-            low_send[at] = total.astype(jnp.bfloat16)
-            return total + source[at].astype(jnp.float32)
-
-        x_send[kind] = lax.fori_loop(0, size, one, x_recv[kind])
-        low_own[pl.ds(rank * share, share)] = low_send[rank]
-
-        @pl.when(team == first_team)
-        def _():
-            team_total(kind).start()
+        lax.fori_loop(1, planes, one, 0)
+
+    def earlier(kind, body):
+        later(1 - min(kind, 1), body)
+
+    def tiles(kind, body):
+        packed, quarter = at_of(kind)[1:]
+
+        def one(i, carry):
+            body(pl.multiple_of(i * TILE, TILE), pl.ds(pl.multiple_of(packed + i * TILE, TILE), TILE))
+            return carry
+
+        lax.fori_loop(0, quarter // TILE, one, 0)
+
+    def own_quarter(kind):
+        base, packed, quarter = at_of(kind)
+        source = st_send if kind == 0 else lg_send
+        a_buf[min(kind, 1), spot, pl.ds(packed, quarter)] = source[pl.ds(base + spot * quarter, quarter)]
+
+    def scan_open(kind):
+        mates(lambda peer: a_copy(kind, peer, spot).start())
+        own_quarter(kind)
+
+    def scan_planes(kind):
+        way = min(kind, 1)
+        mates(lambda peer: a_copy(kind, spot, peer).wait_recv())
+
+        def tile(_, here):
+            total = a_buf[way, 0, here].astype(jnp.float32)
+            for s in range(1, PLANE):
+                total = total + a_buf[way, s, here].astype(jnp.float32)
+            b_send[way, here] = total.astype(jnp.bfloat16)
+
+        tiles(kind, tile)
+        later(kind, lambda plane: b_copy(kind, plane, level).start())
+
+    def scan_close(kind):
+        base, packed, quarter = at_of(kind)
+        way = min(kind, 1)
+        target = prefix if kind == 0 else suffix
+        earlier(kind, lambda plane: b_copy(kind, level, plane).wait_recv())
+
+        def tile(_, here):
+            total = b_buf[way, 0, here].astype(jnp.float32)
+            for z in range(1, planes):
+                total = total + b_buf[way, z, here].astype(jnp.float32)
+            for s in range(PLANE) if kind == 0 else range(PLANE - 1, -1, -1):
+                c_send[way, s, here] = total.astype(jnp.bfloat16)
+                total = total + a_buf[way, s, here].astype(jnp.float32)
+
+        tiles(kind, tile)
+        mates(lambda peer: c_copy(kind, peer, spot).start())
+        target[pl.ds(base + spot * quarter, quarter)] = c_send[way, spot, pl.ds(packed, quarter)]
+
+    def scan_end(kind):
+        mates(lambda peer: c_copy(kind, spot, peer).wait_recv())
+
+    def scan_sent(kind):
+        mates(lambda peer: a_copy(kind, peer, spot).wait_send())
+        later(kind, lambda plane: b_copy(kind, plane, level).wait_send())
+        mates(lambda peer: c_copy(kind, peer, spot).wait_send())
 
     def span_of(c):
         return pl.ds(pl.multiple_of(c * chunk, chunk), chunk)
@@ -346,7 +384,7 @@
             copy.wait_send() if finish else copy.start()
 
     def routed(c):
-        return lax.rem(c, 2) == 1
+        return lax.rem(c, 3) != 0
 
     def pump(phase, c, finish=False):
         def move(j, ways):
@@ -428,7 +466,7 @@
 
     def norm_step(h, carry):
         c = head_cols(h)
-        numerator = normed[h] + contract_mid(q_ref[:, c], prefix[h])
+        numerator = normed[h] + contract_mid(q_ref[:, c], prefix[c])
         inv = 1.0 / jnp.sqrt(jnp.mean(numerator * numerator, axis=-1, keepdims=True) + 1e-06)
         value = numerator * inv
         normed[h] = value
@@ -436,10 +474,8 @@
         att[own_rows, c] = value.astype(jnp.bfloat16)
         return carry
 
-    quarter = width // 4
-
     def att_copy(i):
-        c = pl.ds(i * quarter, quarter)
+        c = span_of(i)
         return pltpu.make_async_remote_copy(
             src_ref=att.at[own_rows, c], dst_ref=att.at[far_rows, c],
             send_sem=t_send_sem.at[i], recv_sem=t_recv_sem.at[i],
@@ -514,19 +550,18 @@
         along = jnp.mean(toward * unit, axis=-1, keepdims=True)
         low = ((toward - unit * along) * inv_spread[h]).astype(jnp.bfloat16)
         ng[:, c] = low
-        lg_send[h] = contract_rows(q_ref[:, c], low).astype(jnp.bfloat16)
+        lg_send[c] = contract_rows(q_ref[:, c], low).astype(jnp.bfloat16)
         return carry
 
     def numer_chunk(c):
         od_copy(c).wait_recv()
         lax.fori_loop(c * chunk_heads, (c + 1) * chunk_heads, numer_step, 0)
-        leave(pair_of(lg_send), slot_of(lg_recv), 2, c)
 
     def pair_step(h, carry):
         c = head_cols(h)
         low = ng[:, c]
         pair = jnp.where(causal, contract_cols(low, v_ref[:, c]), 0.0).astype(jnp.bfloat16)
-        dq_ref[:, c] = (contract_mid(pair, k_ref[:, c]) + contract_cols(low, prefix[h])).astype(jnp.bfloat16)
+        dq_ref[:, c] = (contract_mid(pair, k_ref[:, c]) + contract_cols(low, prefix[c])).astype(jnp.bfloat16)
         k_part[h] = contract_rows(pair, q_ref[:, c])
         v_part[h] = contract_rows(weights[h], low)
         return carry
@@ -538,22 +573,69 @@
 
         lax.fori_loop(0, count, one, 0)
 
-    exchange(pair_of(st_send), slot_of(st_recv), 0, True)
+    def heads_of(c, body):
+        lax.fori_loop(c * chunk_heads, (c + 1) * chunk_heads, body, 0)
+
+    def last_step(h, carry):
+        c = head_cols(h)
+        dk_ref[:, c] = (k_part[h] + contract_cols(v_ref[:, c], suffix[c])).astype(jnp.bfloat16)
+        dv_ref[:, c] = (v_part[h] + contract_mid(k_ref[:, c], suffix[c])).astype(jnp.bfloat16)
+        return carry
+
+    def each(first, last, body):
+        def one(i, carry):
+            body(i)
+            return carry
+
+        lax.fori_loop(first, last, one, 0)
+
+    def aim(group, first, last):
+        def one(c):
+            settle(group, c)
+            direction_step(group, c)
+
+        each(first, last, one)
+
+    e1, e2, e3 = parts[0], parts[0] + parts[1], chunks
+
+    pl.semaphore_wait(barrier, 2 * PLANE - 1)
+    own_piece(0)
     for i in range(half):
         grad_core(i).start()
-        grad_pair(i).start()
-    each(per, own_piece)
-
+    each(0, half // 2, lambda i: grad_pair(i).start())
+    for z in range(planes):
+
+        @pl.when(z >= level)
+        def _():
+            b_buf[0, z] = jnp.zeros(b_buf.shape[2:], b_buf.dtype)
+
+        @pl.when(z <= level)
+        def _():
+            b_buf[1, z] = jnp.zeros(b_buf.shape[2:], b_buf.dtype)
+
+    k_load.wait()
+    v_load.wait()
+    team = heads // PLANE
+
+    def some_states(peer):
+        lax.fori_loop(peer * team, (peer + 1) * team, make_state, 0)
+
+    def open_states(peer):
+        some_states(peer)
+        a_copy(0, peer, spot).start()
+
+    mates(open_states)
+    each(half // 2, half, lambda i: grad_pair(i).start())
+    each(1, e1, own_piece)
+    some_states(spot)
+    own_quarter(0)
     q_load.wait()
-
-    def stage(i):
-        lax.fori_loop(i * (heads // per), (i + 1) * (heads // per), score_step, 0)
-        pump(0, i)
-
-    each(per, stage)
-    arrived(pair_of(st_send), slot_of(st_recv), 0)
-    running(0, 0, st_recv, pre_send, prefix, False)
-    exchange(slot_of(pre_send), pair_of(prefix), 1, True)
+    lax.fori_loop(0, heads, score_step, 0)
+    scan_planes(0)
+    each(0, 2, lambda c: pump(0, c))
+    scan_close(0)
+    each(2, e1, lambda c: pump(0, c))
+    each(0, e1, lambda c: pump(1, c))
     for i in range(half):
         grad_pair(i).wait_recv()
         grad_relay(i).start()
@@ -561,87 +643,90 @@
     for i in range(half):
         own_grad(i).wait()
         grad_core(i).wait_recv()
-    each(per, lambda i: pump(1, i))
+    scan_end(0)
+
+    def stage(c):
+        heads_of(c, norm_step)
+        att_copy(c).start()
+
+    each(0, 4, stage)
+    each(0, e1, lambda c: pump(2, c))
+    each(e1, e2, own_piece)
     for i in range(half):
         grad_relay(i).wait_recv()
-
-    def stage(i):
-        settle(0, i)
-        direction_step(0, i)
-
-    each(per, stage)
-    arrived(slot_of(pre_send), pair_of(prefix), 1)
-
-    def stage(i):
-        lax.fori_loop(i * (heads // per), (i + 1) * (heads // per), norm_step, 0)
-        att_copy(i).start()
-        pump(2, i)
-        settle(1, i)
-        direction_step(1, i)
-
-    for i in range(per):
-        stage(i)
-    each(per, lambda i: own_piece(per + i))
-
-    def stage(i):
-        settle(2, i)
-        direction_step(2, i)
-
-    each(per, stage)
-
-    def stage(i):
-        settle(3, i)
-        direction_step(3, i)
-
-    each(per, stage)
-
-    def stage(i):
-        pump(0, per + i)
-        numer_chunk(i)
-
-    each(per, stage)
-    for i in range(4):
-        att_copy(i).wait_recv()
-
-    def stage(i):
-        pump(1, per + i)
-        settle(0, per + i)
-        direction_step(0, per + i)
-        lax.fori_loop(i * chunk_heads, (i + 1) * chunk_heads, pair_step, 0)
-
-    each(per, stage)
-    for j in groups[0]:
+    each(4, chunks, lambda c: heads_of(c, norm_step))
+    aim(0, 0, e1)
+    aim(1, 0, e1)
+    aim(2, 0, e1)
+    aim(3, 0, e1)
+
+    def stage(c):
+        pump(0, c)
+        att_copy(c - e1 + 4).start()
+
+    each(e1, e2, stage)
+    each(e2, e3, own_piece)
+    each(e2 - e1 + 4, chunks, lambda c: att_copy(c).start())
+    each(0, e1, numer_chunk)
+    scan_open(1)
+    each(e2, e3, lambda c: pump(0, c))
+
+    def stage(c):
+        pump(1, c)
+        settle(0, c)
+        direction_step(0, c)
+        heads_of(c - e1, pair_step)
+
+    each(e1, e2, stage)
+    scan_planes(1)
+
+    def stage(c):
+        pump(2, c)
+        settle(1, c)
+        direction_step(1, c)
+
+    each(e1, e2, stage)
+    scan_close(1)
+    aim(2, e1, e2)
+    aim(3, e1, e2)
+    each(e2, e3, lambda c: pump(1, c))
+    each(0, chunks, lambda c: att_copy(c).wait_recv())
+    aim(0, e2, e3)
+    aim(1, e2, e3)
+    for j in groups[0] + (next_other,):
         partial_step(j)
-
-    def stage(i):
-        pump(2, per + i)
-        settle(1, per + i)
-        direction_step(1, per + i)
-
-    each(per, stage)
-    for j in groups[1]:
+    each(e2, e3, lambda c: pump(2, c))
+    each(e1, e2, numer_chunk)
+    scan_open(2)
+    near = level // (planes // 2)
+
+    @pl.when(core == near)
+    def _():
+        lax.fori_loop(0, half, mix_step, 0)
+
+    aim(2, e2, e3)
+    scan_planes(2)
+    aim(3, e2, e3)
+    scan_close(2)
+    for j in (o2, o3, c2, c3):
         partial_step(j)
-
-    def stage(i):
-        settle(2, per + i)
-        direction_step(2, per + i)
-
-    each(per, stage)
-
-    def stage(i):
-        settle(3, per + i)
-        direction_step(3, per + i)
-
-    each(per, stage)
-    for j in groups[2] + groups[3]:
-        partial_step(j)
-    each(per, lambda i: numer_chunk(per + i))
-    lg_recv[rank] = lg_send[pl.ds(rank * share, share)]
-    lax.fori_loop(0, half, mix_step, 0)
-    arrived(pair_of(lg_send), slot_of(lg_recv), 2)
-    running(1, 1, lg_recv, suf_send, suffix, True)
-    exchange(slot_of(suf_send), pair_of(suffix), 3, True)
-    lax.fori_loop(heads // 2, heads, pair_step, 0)
+    each(e2, e3, numer_chunk)
+    scan_open(3)
+    each(e1, e2, lambda c: heads_of(c, pair_step))
+    scan_planes(3)
+
+    @pl.when(core != near)
+    def _():
+        lax.fori_loop(0, half, mix_step, 0)
+
+    each(e2, e3, lambda c: heads_of(c, pair_step))
+    scan_end(1)
+    scan_close(3)
+    each(0, e1, lambda c: heads_of(c, last_step))
+    scan_end(2)
+    each(e1, e2, lambda c: heads_of(c, last_step))
+    scan_end(3)
+    each(e2, e3, lambda c: heads_of(c, last_step))
 
     def take_mixed(slot, carry):
         m_copy(slot).wait_recv()
@@ -649,40 +734,23 @@
         return carry
 
     lax.fori_loop(0, half, take_mixed, 0)
-    arrived(slot_of(suf_send), pair_of(suffix), 3)
-
-    def last_step(h, carry):
-        c = head_cols(h)
-        dk_ref[:, c] = (k_part[h] + contract_cols(v_ref[:, c], suffix[h])).astype(jnp.bfloat16)
-        dv_ref[:, c] = (v_part[h] + contract_mid(k_ref[:, c], suffix[h])).astype(jnp.bfloat16)
-        return carry
-
-    lax.fori_loop(0, heads, last_step, 0)
 
     def finish(c):
         own_piece(c, True)
         for phase in range(3):
             pump(phase, c, True)
         od_copy(c).wait_send()
-
-    each(chunks, finish)
+        att_copy(c).wait_send()
+
+    each(0, chunks, finish)
 
     def finish(i):
         for copy in (grad_core(i), grad_pair(i), grad_relay(i), p_copy(i), m_copy(i)):
             copy.wait_send()
 
-    each(half, finish)
-    for i in range(4):
-        att_copy(i).wait_send()
-    exchange(pair_of(st_send), slot_of(st_recv), 0, False)
-    exchange(slot_of(pre_send), pair_of(prefix), 1, False)
-    exchange(pair_of(lg_send), slot_of(lg_recv), 2, False)
-    exchange(slot_of(suf_send), pair_of(suffix), 3, False)
-    for kind in range(2):
-
-        @pl.when(team == kind)
-        def _():
-            team_total(kind).wait_send()
+    each(0, half, finish)
+    for kind in range(len(parts) + 1):
+        scan_sent(kind)
 
 
 def store_kernel(*refs):
@@ -713,11 +781,10 @@
     low, wide = jnp.bfloat16, jnp.float32
     size = blocks // 2
     half = size // 2
-    share = heads // size
-    chunks = CHUNKS
-    state = pltpu.VMEM((heads, HEAD_DIM, HEAD_DIM), low)
-    slots = pltpu.VMEM((size, share, HEAD_DIM, HEAD_DIM), low)
-    totals = pltpu.VMEM((2, share, HEAD_DIM, HEAD_DIM), wide)
+    chunks = sum(PARTS)
+    state = pltpu.VMEM((rows, HEAD_DIM), low)
+    fourth = rows // PLANE
+    by_spot = pltpu.VMEM((2, PLANE, fourth, HEAD_DIM), low)
     by_head = pltpu.VMEM((heads, length, HEAD_DIM), wide)
     flat = pltpu.VMEM((length, width), low)
     parts = pltpu.VMEM((half, 2 * length, cols), low)
@@ -727,8 +794,9 @@
     out = jax.ShapeDtypeStruct((length, width), low)
     vmem, in_hbm = pl.BlockSpec(memory_space=pltpu.VMEM), pl.BlockSpec(memory_space=pltpu.HBM)
     pieces = dma((size, chunks))
+    scans = dma((len(PARTS) + 1, PLANE))
     results = pl.pallas_call(
-        functools.partial(kernel, blocks, chunks),
+        functools.partial(kernel, blocks, chunks, PARTS),
         out_shape=(out, out, out, out),
         in_specs=[in_hbm] * 5,
         out_specs=(vmem, vmem, vmem, vmem),
@@ -736,7 +804,8 @@
             flat, flat, flat,
             pltpu.VMEM((size, rows, cols), low),
             pltpu.VMEM((size, 2 * length, cols), low),
-            state, slots, slots, state, state, slots, slots, state,
+            state, state, state, state,
+            by_spot, pltpu.VMEM((2, fourth, HEAD_DIM), low), by_spot, by_spot,
             pltpu.VMEM((2 * length, rows), wide),
             steps, steps,
             by_head, by_head,
@@ -744,15 +813,14 @@
             pltpu.VMEM((2 * length, width), low),
             parts, parts, parts, shares, shares,
             flat, by_head, by_head,
-            totals, totals,
             pieces, pieces, pieces, pieces,
-            dma((4 + half,)), dma((3, half)), dma((3, half)), dma((4, blocks)), dma((4, blocks)),
-            dma((half,)), dma((half,)), dma((half,)), dma((half,)), dma((4,)), dma((4,)),
+            dma((4 + half,)), dma((3, half)), dma((3, half)),
+            scans, scans, scans, scans, scans, scans,
+            dma((half,)), dma((half,)), dma((half,)), dma((half,)), dma((chunks,)), dma((chunks,)),
             dma((chunks,)), dma((chunks,)),
-            dma((2,)), dma((2,)),
         ],
         compiler_params=pltpu.CompilerParams(
-            collective_id=0, has_side_effects=True, vmem_limit_bytes=44 * 2**20
+            collective_id=0, has_side_effects=True, vmem_limit_bytes=49 * 2**20
         ),
     )(queries, key_rows, values, out_weight, out_grad)
     return store(*results)

time: 152 us -> 139 us (0.914)
  Pallas kernels: 145 us -> 138 us
  local copies, waits for them, and re-layouts: 6.11 us -> 0 us
    pallas_call x1, Pallas kernels: 143 us -> 136 us  [fused(): pl.pallas_call(functools.partial(kernel, blocks, chunks, PARTS), out_shap...]
    unnamed x10 -> x0, local copies, waits for them, and re-layouts: 6.11 us -> none
where the time goes in v2:
time: 139 us
  Pallas kernels  138 us (99%)
    pallas_call x1, Pallas kernels, fused(): pl.pallas_call(functools.partial(kernel, blocks, chunks, PARTS), out_shap...  136 us

profile of v2, /device:TPU:0, one launch (start us, length us, event | category | flops | bytes accessed | tf_op | source)
XLA Modules:
  0.0 138.9 jit_solution(14134868454114451391)
XLA Ops:
  0.6 136.2 %shard_map.84 = (bf16[256,2048]{1,0:T(8,128)(2,1)S(1)}, bf16[256,2048]{1,0:T(8,128)(2,1)S(1)}, bf16[256,2048]{1,0:T(8,128)(2,1)S(1)}, bf16[256,2048]{1,0:T(8,128)(2,1)S(1)}) custom-call(bf16[256,2048]{1,0:T(8,128)(2,1)} %q_in.1, bf16[256,2048]{1,0:T(8,128)(2,1)} %k_in.1, bf16[256,2048]{1,0:T(8,128)(2,1)} %v_in.1, bf16[2048,256]{1,0:T(8,128)(2,1)} %w_ref.1, ...), custom_call_target="tpu_custom_call" | custom-call | tf_op jit(solution)/shard_map/pallas_call | solution.py:798
  136.8 2.0 %shard_map.85 = (bf16[256,2048]{1,0:T(8,128)(2,1)}, bf16[256,2048]{1,0:T(8,128)(2,1)}, bf16[256,2048]{1,0:T(8,128)(2,1)}, bf16[256,2048]{1,0:T(8,128)(2,1)}) custom-call(bf16[256,2048]{1,0:T(8,128)(2,1)S(1)} %get-tuple-element.8.refs_0_, bf16[256,2048]{1,0:T(8,128)(2,1)S(1)} %get-tuple-element.9.refs_1_, bf16[256,2048]{1,0:T(8,128)(2,1)S(1)} %get-tuple-element.10.refs_2_, ...), custom_call_target="tpu_custom_call" | custom-call | tf_op jit(solution)/shard_map/pallas_call | solution.py:767

commit v3 on v2

--- a/solution.py
+++ b/solution.py
@@ -133,9 +133,9 @@
     q_ref, k_ref, v_ref, w_all, g_all, st_send, prefix, lg_send, suffix, a_buf, b_send, b_buf, c_send,
     out_dir, od_send, od_recv, normed, inv_spread, weights, att, p_own, p_send, p_recv, m_send, m_recv,
     ng, k_part, v_part,
-    w_recv_sem, wy_sem, wi_sem, wo_sem, local_sem, g_send_sem, g_recv_sem,
+    w_recv_sem, w_send_sem, local_sem, g_send_sem, g_recv_sem,
     a_send_sem, a_recv_sem, b_send_sem, b_recv_sem, c_send_sem, c_recv_sem,
-    p_send_sem, p_recv_sem, m_send_sem, m_recv_sem, t_send_sem, t_recv_sem, o_send_sem, o_recv_sem,
+    p_send_sem, p_recv_sem, m_sem, t_sem, o_send_sem, o_recv_sem,
 ):
     me = lax.axis_index("seq")
     core = lax.axis_index("head")
@@ -194,18 +194,26 @@
     half = size // 2
     own_rows, far_rows = pl.ds(0, length), pl.ds(length, length)
 
+    def bulk(ref, sent=None, got=None):
+        copy = pltpu.make_async_remote_copy(
+            src_ref=ref, dst_ref=ref,
+            send_sem=got if sent is None else sent, recv_sem=sent if got is None else got,
+            device_id=(me, other), device_id_type=MESH,
+        )
+        copy.wait_recv() if sent is None else copy.wait_send()
+
     def grad_cols(j, parity):
         return pl.ds(pl.multiple_of((lax.rem(j, half) * 2 + parity) * cols, cols), cols)
 
     def own_grad(i):
         j = core * half + i
-        return pltpu.make_async_copy(g_ref.at[:, grad_cols(j, bit_x)], g_all.at[j, own_rows], local_sem.at[4 + i])
+        return pltpu.make_async_copy(g_ref.at[:, grad_cols(j, bit_x)], g_all.at[j, own_rows], local_sem.at[4])
 
     def grad_core(i):
         j = core * half + i
         return pltpu.make_async_remote_copy(
             src_ref=g_ref.at[:, grad_cols(j, bit_x)], dst_ref=g_all.at[j, own_rows],
-            send_sem=g_send_sem.at[0, i], recv_sem=g_recv_sem.at[0, i],
+            send_sem=g_send_sem.at[0], recv_sem=g_recv_sem.at[0],
             device_id=(me, other), device_id_type=MESH,
         )
 
@@ -213,7 +221,7 @@
         j = core * half + i
         return pltpu.make_async_remote_copy(
             src_ref=g_ref.at[:, grad_cols(j, 1 - bit_x)], dst_ref=g_all.at[j, far_rows],
-            send_sem=g_send_sem.at[1, i], recv_sem=g_recv_sem.at[1, i],
+            send_sem=g_send_sem.at[1], recv_sem=g_recv_sem.at[1],
             device_id=at_seq(nbr_x), device_id_type=MESH,
         )
 
@@ -221,7 +229,7 @@
         j = core * half + i
         return pltpu.make_async_remote_copy(
             src_ref=g_all.at[j, far_rows], dst_ref=g_all.at[j, far_rows],
-            send_sem=g_send_sem.at[2, i], recv_sem=g_recv_sem.at[2, i],
+            send_sem=g_send_sem.at[2], recv_sem=g_recv_sem.at[2],
             device_id=(me, other), device_id_type=MESH,
         )
 
@@ -248,7 +256,7 @@
         return pltpu.make_async_remote_copy(
             src_ref=source.at[pl.ds(base + peer * quarter, quarter)],
             dst_ref=a_buf.at[min(kind, 1), sender, pl.ds(packed, quarter)],
-            send_sem=a_send_sem.at[kind, peer], recv_sem=a_recv_sem.at[kind, sender],
+            send_sem=a_send_sem.at[kind], recv_sem=a_recv_sem.at[kind],
             device_id=at_seq(level * PLANE + peer), device_id_type=MESH,
         )
 
@@ -257,7 +265,7 @@
         return pltpu.make_async_remote_copy(
             src_ref=b_send.at[min(kind, 1), pl.ds(packed, quarter)],
             dst_ref=b_buf.at[min(kind, 1), sender, pl.ds(packed, quarter)],
-            send_sem=b_send_sem.at[kind, plane], recv_sem=b_recv_sem.at[kind, sender],
+            send_sem=b_send_sem.at[kind], recv_sem=b_recv_sem.at[kind],
             device_id=at_seq(plane * PLANE + spot), device_id_type=MESH,
         )
 
@@ -267,7 +275,7 @@
         return pltpu.make_async_remote_copy(
             src_ref=c_send.at[min(kind, 1), peer, pl.ds(packed, quarter)],
             dst_ref=target.at[pl.ds(base + sender * quarter, quarter)],
-            send_sem=c_send_sem.at[kind, peer], recv_sem=c_recv_sem.at[kind, sender],
+            send_sem=c_send_sem.at[kind], recv_sem=c_recv_sem.at[kind],
             device_id=at_seq(level * PLANE + peer), device_id_type=MESH,
         )
 
@@ -290,8 +298,11 @@
 
         lax.fori_loop(1, planes, one, 0)
 
-    def earlier(kind, body):
-        later(1 - min(kind, 1), body)
+    def behind(kind):
+        return level if kind == 0 else planes - 1 - level
+
+    def rows_for(kind, count):
+        return st_send.at[pl.ds(0, count * at_of(kind)[2])]
 
     def tiles(kind, body):
         packed, quarter = at_of(kind)[1:]
@@ -313,7 +324,7 @@
 
     def scan_planes(kind):
         way = min(kind, 1)
-        mates(lambda peer: a_copy(kind, spot, peer).wait_recv())
+        bulk(rows_for(kind, PLANE - 1), got=a_recv_sem.at[kind])
 
         def tile(_, here):
             total = a_buf[way, 0, here].astype(jnp.float32)
@@ -328,7 +339,12 @@
         base, packed, quarter = at_of(kind)
         way = min(kind, 1)
         target = prefix if kind == 0 else suffix
-        earlier(kind, lambda plane: b_copy(kind, level, plane).wait_recv())
+        for count in range(1, planes):
+
+            @pl.when(behind(kind) == count)
+            def _():
+                bulk(rows_for(kind, count), got=b_recv_sem.at[kind])
+
 
         def tile(_, here):
             total = b_buf[way, 0, here].astype(jnp.float32)
@@ -343,12 +359,16 @@
         target[pl.ds(base + spot * quarter, quarter)] = c_send[way, spot, pl.ds(packed, quarter)]
 
     def scan_end(kind):
-        mates(lambda peer: c_copy(kind, spot, peer).wait_recv())
+        bulk(rows_for(kind, PLANE - 1), got=c_recv_sem.at[kind])
 
     def scan_sent(kind):
-        mates(lambda peer: a_copy(kind, peer, spot).wait_send())
-        later(kind, lambda plane: b_copy(kind, plane, level).wait_send())
-        mates(lambda peer: c_copy(kind, peer, spot).wait_send())
+        bulk(rows_for(kind, PLANE - 1), sent=a_send_sem.at[kind])
+        bulk(rows_for(kind, PLANE - 1), sent=c_send_sem.at[kind])
+        for count in range(1, planes):
+
+            @pl.when(planes - 1 - behind(kind) == count)
+            def _():
+                bulk(rows_for(kind, count), sent=b_send_sem.at[kind])
 
     def span_of(c):
         return pl.ds(pl.multiple_of(c * chunk, chunk), chunk)
@@ -358,41 +378,37 @@
         return pltpu.make_async_remote_copy(
             src_ref=w_ref.at[span] if own else w_all.at[j, span],
             dst_ref=w_all.at[j, span],
-            send_sem=sems.at[j, c], recv_sem=w_recv_sem.at[j, c],
+            send_sem=sems, recv_sem=w_recv_sem.at[j, c],
             device_id=at_seq(target), device_id_type=MESH,
         )
 
-    def to_y(j, c, own=False):
-        return piece(j, c, wy_sem, nbr_y, own)
+    def to_y(j, c, own=False, slot=0):
+        return piece(j, c, w_send_sem.at[slot], nbr_y, own)
 
     def to_inner(j, c, own=False):
-        return piece(j, c, wi_sem, inner, own)
-
-    def to_outer(j, c, own=False):
-        return piece(j, c, wo_sem, outer, own)
+        return piece(j, c, w_send_sem.at[1], inner, own)
+
+    def to_outer(j, c, own=False, slot=2):
+        return piece(j, c, w_send_sem.at[slot], outer, own)
 
     def landed(j, c):
         to_y(j, c).wait_recv()
 
-    def own_piece(c, finish=False):
-        for copy in (to_y(mine, c, True), to_inner(mine, c, True)):
-            copy.wait_send() if finish else copy.start()
+    def own_piece(c):
+        to_y(mine, c, True).start()
+        to_inner(mine, c, True).start()
 
         @pl.when(middle)
         def _():
-            copy = to_outer(mine, c, True)
-            copy.wait_send() if finish else copy.start()
-
-    def routed(c):
-        return lax.rem(c, 3) != 0
-
-    def pump(phase, c, finish=False):
+            to_outer(mine, c, True).start()
+
+    turn = parts[0] + parts[1]
+
+    def pump(phase, c):
         def move(j, ways):
-            if not finish:
-                landed(j, c)
+            landed(j, c)
             for way in ways:
-                copy = way(j, c)
-                copy.wait_send() if finish else copy.start()
+                way(j, c).start()
 
         if phase == 0:
 
@@ -420,23 +436,32 @@
 
             @pl.when(edge)
             def _():
-                if not finish:
-                    landed(o3, c)
-
-                @pl.when(jnp.logical_not(routed(c)))
+                landed(o3, c)
+
+                @pl.when(c == turn)
                 def _():
-                    copy = to_y(o3, c)
-                    copy.wait_send() if finish else copy.start()
+                    to_y(o3, c, slot=3).start()
 
             @pl.when(middle)
             def _():
-                if not finish:
-                    landed(c3, c)
-
-                @pl.when(routed(c))
+                landed(c3, c)
+
+                @pl.when(c != turn)
                 def _():
-                    copy = to_outer(c3, c)
-                    copy.wait_send() if finish else copy.start()
+                    to_outer(c3, c, slot=3).start()
+
+    def pieces_sent():
+        bulk(w_all.at[pl.ds(0, 3)], sent=w_send_sem.at[0])
+        bulk(w_all.at[pl.ds(0, 2)], sent=w_send_sem.at[1])
+
+        @pl.when(middle)
+        def _():
+            bulk(w_all.at[pl.ds(0, 3)], sent=w_send_sem.at[2])
+            bulk(w_all.at[0, pl.ds(0, (chunks - 1) * chunk)], sent=w_send_sem.at[3])
+
+        @pl.when(edge)
+        def _():
+            bulk(w_all.at[0, pl.ds(0, chunk)], sent=w_send_sem.at[3])
 
     def settle(group, c):
         if group == 0:
@@ -478,14 +503,14 @@
         c = span_of(i)
         return pltpu.make_async_remote_copy(
             src_ref=att.at[own_rows, c], dst_ref=att.at[far_rows, c],
-            send_sem=t_send_sem.at[i], recv_sem=t_recv_sem.at[i],
+            send_sem=t_sem.at[0], recv_sem=t_sem.at[1],
             device_id=at_seq(nbr_x), device_id_type=MESH,
         )
 
     def od_copy(c):
         return pltpu.make_async_remote_copy(
             src_ref=od_send.at[c], dst_ref=od_recv.at[c],
-            send_sem=o_send_sem.at[c], recv_sem=o_recv_sem.at[c],
+            send_sem=o_send_sem.at[0], recv_sem=o_recv_sem.at[c],
             device_id=at_seq(nbr_x), device_id_type=MESH,
         )
 
@@ -507,14 +532,14 @@
     def p_copy(slot):
         return pltpu.make_async_remote_copy(
             src_ref=p_send.at[slot], dst_ref=p_recv.at[slot],
-            send_sem=p_send_sem.at[slot], recv_sem=p_recv_sem.at[slot],
+            send_sem=p_send_sem.at[0], recv_sem=p_recv_sem.at[slot],
             device_id=(me, other), device_id_type=MESH,
         )
 
     def m_copy(slot):
         return pltpu.make_async_remote_copy(
             src_ref=m_send.at[slot], dst_ref=m_recv.at[slot],
-            send_sem=m_send_sem.at[slot], recv_sem=m_recv_sem.at[slot],
+            send_sem=m_sem.at[0], recv_sem=m_sem.at[1],
             device_id=at_seq(nbr_x), device_id_type=MESH,
         )
 
@@ -602,7 +627,7 @@
     own_piece(0)
     for i in range(half):
         grad_core(i).start()
-    each(0, half // 2, lambda i: grad_pair(i).start())
+    grad_pair(0).start()
     for z in range(planes):
 
         @pl.when(z >= level)
@@ -625,24 +650,24 @@
         a_copy(0, peer, spot).start()
 
     mates(open_states)
-    each(half // 2, half, lambda i: grad_pair(i).start())
+    each(1, half, lambda i: grad_pair(i).start())
     each(1, e1, own_piece)
     some_states(spot)
     own_quarter(0)
     q_load.wait()
     lax.fori_loop(0, heads, score_step, 0)
     scan_planes(0)
-    each(0, 2, lambda c: pump(0, c))
+    pump(0, 0)
     scan_close(0)
-    each(2, e1, lambda c: pump(0, c))
+    each(1, e1, lambda c: pump(0, c))
     each(0, e1, lambda c: pump(1, c))
+    some_grads = g_all.at[pl.ds(0, half), own_rows]
+    bulk(some_grads, got=g_recv_sem.at[1])
     for i in range(half):
-        grad_pair(i).wait_recv()
         grad_relay(i).start()
     own_w.wait()
-    for i in range(half):
-        own_grad(i).wait()
-        grad_core(i).wait_recv()
+    pltpu.make_async_copy(some_grads, some_grads, local_sem.at[4]).wait()
+    bulk(some_grads, got=g_recv_sem.at[0])
     scan_end(0)
 
     def stage(c):
@@ -652,8 +677,7 @@
     each(0, 4, stage)
     each(0, e1, lambda c: pump(2, c))
     each(e1, e2, own_piece)
-    for i in range(half):
-        grad_relay(i).wait_recv()
+    bulk(some_grads, got=g_recv_sem.at[2])
     each(4, chunks, lambda c: heads_of(c, norm_step))
     aim(0, 0, e1)
     aim(1, 0, e1)
@@ -679,76 +703,71 @@
 
     each(e1, e2, stage)
     scan_planes(1)
-
-    def stage(c):
-        pump(2, c)
-        settle(1, c)
-        direction_step(1, c)
-
-    each(e1, e2, stage)
-    scan_close(1)
-    aim(2, e1, e2)
-    aim(3, e1, e2)
-    each(e2, e3, lambda c: pump(1, c))
-    each(0, chunks, lambda c: att_copy(c).wait_recv())
+    bulk(att.at[own_rows], got=t_sem.at[1])
     aim(0, e2, e3)
-    aim(1, e2, e3)
-    for j in groups[0] + (next_other,):
-        partial_step(j)
-    each(e2, e3, lambda c: pump(2, c))
-    each(e1, e2, numer_chunk)
-    scan_open(2)
+    partial_step(mine)
+    partial_step(near_own)
+    partial_step(near_other)
+    aim(1, e1, e2)
+    each(e2, e3, lambda c: settle(1, c))
+    partial_step(next_other)
+    pump(2, e1)
     near = level // (planes // 2)
 
     @pl.when(core == near)
     def _():
         lax.fori_loop(0, half, mix_step, 0)
 
+    each(e1 + 1, e2 - 1, lambda c: pump(2, c))
+    scan_close(1)
+    each(e2 - 1, e2, lambda c: pump(2, c))
+    each(e2, e3, lambda c: pump(1, c))
+    each(e2, e3, lambda c: direction_step(1, c))
+    partial_step(o2)
+    aim(2, e1, e2)
+    aim(3, e1, e2)
+    scan_end(1)
+    each(0, e1, lambda c: heads_of(c, last_step))
+    each(e2, e3, lambda c: pump(2, c))
     aim(2, e2, e3)
-    scan_planes(2)
+    partial_step(o3)
     aim(3, e2, e3)
-    scan_close(2)
-    for j in (o2, o3, c2, c3):
-        partial_step(j)
+    each(e1, e2, numer_chunk)
+    scan_open(2)
+    partial_step(c2)
     each(e2, e3, numer_chunk)
     scan_open(3)
-    each(e1, e2, lambda c: heads_of(c, pair_step))
+    partial_step(c3)
+    scan_planes(2)
     scan_planes(3)
 
     @pl.when(core != near)
     def _():
         lax.fori_loop(0, half, mix_step, 0)
 
+    scan_close(2)
+    each(e1, e2, lambda c: heads_of(c, pair_step))
+    scan_close(3)
     each(e2, e3, lambda c: heads_of(c, pair_step))
-    scan_end(1)
-    scan_close(3)
-    each(0, e1, lambda c: heads_of(c, last_step))
     scan_end(2)
     each(e1, e2, lambda c: heads_of(c, last_step))
     scan_end(3)
     each(e2, e3, lambda c: heads_of(c, last_step))
 
     def take_mixed(slot, carry):
-        m_copy(slot).wait_recv()
         mixed_ref[:, mixed_cols(slot, 1 - bit_x)] = m_recv[slot]
         return carry
 
+    bulk(m_recv, got=m_sem.at[1])
     lax.fori_loop(0, half, take_mixed, 0)
 
-    def finish(c):
-        own_piece(c, True)
-        for phase in range(3):
-            pump(phase, c, True)
-        od_copy(c).wait_send()
-        att_copy(c).wait_send()
-
-    each(0, chunks, finish)
-
-    def finish(i):
-        for copy in (grad_core(i), grad_pair(i), grad_relay(i), p_copy(i), m_copy(i)):
-            copy.wait_send()
-
-    each(0, half, finish)
+    pieces_sent()
+    bulk(od_send, sent=o_send_sem.at[0])
+    bulk(att.at[own_rows], sent=t_sem.at[0])
+    bulk(p_send, sent=p_send_sem.at[0])
+    bulk(m_send, sent=m_sem.at[0])
+    for i in range(3):
+        bulk(some_grads, sent=g_send_sem.at[i])
     for kind in range(len(parts) + 1):
         scan_sent(kind)
 
@@ -793,8 +812,7 @@
     dma = pltpu.SemaphoreType.DMA
     out = jax.ShapeDtypeStruct((length, width), low)
     vmem, in_hbm = pl.BlockSpec(memory_space=pltpu.VMEM), pl.BlockSpec(memory_space=pltpu.HBM)
-    pieces = dma((size, chunks))
-    scans = dma((len(PARTS) + 1, PLANE))
+    scans = dma((len(PARTS) + 1,))
     results = pl.pallas_call(
         functools.partial(kernel, blocks, chunks, PARTS),
         out_shape=(out, out, out, out),
@@ -813,11 +831,9 @@
             pltpu.VMEM((2 * length, width), low),
             parts, parts, parts, shares, shares,
             flat, by_head, by_head,
-            pieces, pieces, pieces, pieces,
-            dma((4 + half,)), dma((3, half)), dma((3, half)),
+            dma((size, chunks)), dma((4,)), dma((5,)), dma((3,)), dma((3,)),
             scans, scans, scans, scans, scans, scans,
-            dma((half,)), dma((half,)), dma((half,)), dma((half,)), dma((chunks,)), dma((chunks,)),
-            dma((chunks,)), dma((chunks,)),
+            dma((1,)), dma((half,)), dma((2,)), dma((2,)), dma((1,)), dma((chunks,)),
         ],
         compiler_params=pltpu.CompilerParams(
             collective_id=0, has_side_effects=True, vmem_limit_bytes=49 * 2**20

time: 139 us -> 130 us (0.935)
  Pallas kernels: 138 us -> 129 us
    pallas_call x1, Pallas kernels: 136 us -> 127 us  [fused(): pl.pallas_call(functools.partial(kernel, blocks, chunks, PARTS), out_shap...]
where the time goes in v3:
time: 130 us; the launch traced here: 129 us
  Pallas kernels  129 us (99%)
    pallas_call x1, Pallas kernels, fused(): pl.pallas_call(functools.partial(kernel, blocks, chunks, PARTS), out_shap...  127 us

profile of v3, /device:TPU:0, one launch (start us, length us, event | category | flops | bytes accessed | tf_op | source)
XLA Modules:
  0.0 129.4 jit_solution(1378967987285238207)
XLA Ops:
  0.6 126.7 %shard_map.84 = (bf16[256,2048]{1,0:T(8,128)(2,1)S(1)}, bf16[256,2048]{1,0:T(8,128)(2,1)S(1)}, bf16[256,2048]{1,0:T(8,128)(2,1)S(1)}, bf16[256,2048]{1,0:T(8,128)(2,1)S(1)}) custom-call(bf16[256,2048]{1,0:T(8,128)(2,1)} %q_in.1, bf16[256,2048]{1,0:T(8,128)(2,1)} %k_in.1, bf16[256,2048]{1,0:T(8,128)(2,1)} %v_in.1, bf16[2048,256]{1,0:T(8,128)(2,1)} %w_ref.1, ...), custom_call_target="tpu_custom_call" | custom-call | tf_op jit(solution)/shard_map/pallas_call | solution.py:816
  127.4 2.0 %shard_map.85 = (bf16[256,2048]{1,0:T(8,128)(2,1)}, bf16[256,2048]{1,0:T(8,128)(2,1)}, bf16[256,2048]{1,0:T(8,128)(2,1)}, bf16[256,2048]{1,0:T(8,128)(2,1)}) custom-call(bf16[256,2048]{1,0:T(8,128)(2,1)S(1)} %get-tuple-element.8.refs_0_, bf16[256,2048]{1,0:T(8,128)(2,1)S(1)} %get-tuple-element.9.refs_1_, bf16[256,2048]{1,0:T(8,128)(2,1)S(1)} %get-tuple-element.10.refs_2_, ...), custom_call_target="tpu_custom_call" | custom-call | tf_op jit(solution)/shard_map/pallas_call | solution.py:786

commit v4 on v3

--- a/solution.py
+++ b/solution.py
@@ -12,6 +12,8 @@
 PLANE = 4
 PARTS = (3, 3, 2)
 TILE = 64
+FOLDED = 1
+EARLY = 2
 
 
 def prefix_2(value, axis, combine, identity):
@@ -288,7 +290,7 @@
 
     def later(kind, body):
         def one(i, carry):
-            plane = level + i if kind == 0 else level - i
+            plane = level + i if kind == 0 else level - planes + i
 
             @pl.when(jnp.logical_and(plane >= 0, plane < planes))
             def _():
@@ -402,7 +404,10 @@
         def _():
             to_outer(mine, c, True).start()
 
-    turn = parts[0] + parts[1]
+    turns = parts[0], parts[0] + parts[1]
+
+    def by_y(c):
+        return jnp.logical_or(c == turns[0], c == turns[1])
 
     def pump(phase, c):
         def move(j, ways):
@@ -438,7 +443,7 @@
             def _():
                 landed(o3, c)
 
-                @pl.when(c == turn)
+                @pl.when(by_y(c))
                 def _():
                     to_y(o3, c, slot=3).start()
 
@@ -446,7 +451,7 @@
             def _():
                 landed(c3, c)
 
-                @pl.when(c != turn)
+                @pl.when(jnp.logical_not(by_y(c)))
                 def _():
                     to_outer(c3, c, slot=3).start()
 
@@ -457,11 +462,11 @@
         @pl.when(middle)
         def _():
             bulk(w_all.at[pl.ds(0, 3)], sent=w_send_sem.at[2])
-            bulk(w_all.at[0, pl.ds(0, (chunks - 1) * chunk)], sent=w_send_sem.at[3])
+            bulk(w_all.at[0, pl.ds(0, (chunks - len(turns)) * chunk)], sent=w_send_sem.at[3])
 
         @pl.when(edge)
         def _():
-            bulk(w_all.at[0, pl.ds(0, chunk)], sent=w_send_sem.at[3])
+            bulk(w_all.at[0, pl.ds(0, len(turns) * chunk)], sent=w_send_sem.at[3])
 
     def settle(group, c):
         if group == 0:
@@ -661,6 +666,7 @@
     scan_close(0)
     each(1, e1, lambda c: pump(0, c))
     each(0, e1, lambda c: pump(1, c))
+    each(e1, e2, own_piece)
     some_grads = g_all.at[pl.ds(0, half), own_rows]
     bulk(some_grads, got=g_recv_sem.at[1])
     for i in range(half):
@@ -676,7 +682,6 @@
 
     each(0, 4, stage)
     each(0, e1, lambda c: pump(2, c))
-    each(e1, e2, own_piece)
     bulk(some_grads, got=g_recv_sem.at[2])
     each(4, chunks, lambda c: heads_of(c, norm_step))
     aim(0, 0, e1)
@@ -735,20 +740,32 @@
     each(e1, e2, numer_chunk)
     scan_open(2)
     partial_step(c2)
+
+    def far_mix(*blocks_done):
+        @pl.when(core != near)
+        def _():
+            for j in blocks_done:
+                mix_step(lax.rem(j, half), 0)
+
     each(e2, e3, numer_chunk)
     scan_open(3)
+    far_mix(o2, o3)
     partial_step(c3)
     scan_planes(2)
     scan_planes(3)
 
-    @pl.when(core != near)
+    @pl.when(level == planes - 1)
     def _():
-        lax.fori_loop(0, half, mix_step, 0)
-
-    scan_close(2)
-    each(e1, e2, lambda c: heads_of(c, pair_step))
-    scan_close(3)
-    each(e2, e3, lambda c: heads_of(c, pair_step))
+        scan_close(2)
+        scan_close(3)
+
+    far_mix(c2, c3)
+    each(e1, e3, lambda c: heads_of(c, pair_step))
+    @pl.when(level < planes - 1)
+    def _():
+        scan_close(2)
+        scan_close(3)
+
     scan_end(2)
     each(e1, e2, lambda c: heads_of(c, last_step))
     scan_end(3)

time: 130 us -> 128 us (0.985)
  no operation moved by 1% of the time
where the time goes in v4:
time: 128 us
  Pallas kernels  128 us (100%)
    pallas_call x1, Pallas kernels, fused(): pl.pallas_call(functools.partial(kernel, blocks, chunks, PARTS), out_shap...  125 us

profile of v4, /device:TPU:0, one launch (start us, length us, event | category | flops | bytes accessed | tf_op | source)
XLA Modules:
  0.0 128.2 jit_solution(4140707604177249571)
XLA Ops:
  0.6 125.5 %shard_map.84 = (bf16[256,2048]{1,0:T(8,128)(2,1)S(1)}, bf16[256,2048]{1,0:T(8,128)(2,1)S(1)}, bf16[256,2048]{1,0:T(8,128)(2,1)S(1)}, bf16[256,2048]{1,0:T(8,128)(2,1)S(1)}) custom-call(bf16[256,2048]{1,0:T(8,128)(2,1)} %q_in.1, bf16[256,2048]{1,0:T(8,128)(2,1)} %k_in.1, bf16[256,2048]{1,0:T(8,128)(2,1)} %v_in.1, bf16[2048,256]{1,0:T(8,128)(2,1)} %w_ref.1, ...), custom_call_target="tpu_custom_call" | custom-call | tf_op jit(solution)/shard_map/pallas_call | solution.py:833
  126.1 2.0 %shard_map.85 = (bf16[256,2048]{1,0:T(8,128)(2,1)}, bf16[256,2048]{1,0:T(8,128)(2,1)}, bf16[256,2048]{1,0:T(8,128)(2,1)}, bf16[256,2048]{1,0:T(8,128)(2,1)}) custom-call(bf16[256,2048]{1,0:T(8,128)(2,1)S(1)} %get-tuple-element.8.refs_0_, bf16[256,2048]{1,0:T(8,128)(2,1)S(1)} %get-tuple-element.9.refs_1_, bf16[256,2048]{1,0:T(8,128)(2,1)S(1)} %get-tuple-element.10.refs_2_, ...), custom_call_target="tpu_custom_call" | custom-call | tf_op jit(solution)/shard_map/pallas_call | solution.py:803

commit v5 on v4

--- a/solution.py
+++ b/solution.py
@@ -404,10 +404,10 @@
         def _():
             to_outer(mine, c, True).start()
 
-    turns = parts[0], parts[0] + parts[1]
+    turns = 0, parts[0], parts[0] + parts[1]
 
     def by_y(c):
-        return jnp.logical_or(c == turns[0], c == turns[1])
+        return jnp.logical_or(c == turns[0], jnp.logical_or(c == turns[1], c == turns[2]))
 
     def pump(phase, c):
         def move(j, ways):
@@ -731,8 +731,6 @@
     partial_step(o2)
     aim(2, e1, e2)
     aim(3, e1, e2)
-    scan_end(1)
-    each(0, e1, lambda c: heads_of(c, last_step))
     each(e2, e3, lambda c: pump(2, c))
     aim(2, e2, e3)
     partial_step(o3)
@@ -740,6 +738,9 @@
     each(e1, e2, numer_chunk)
     scan_open(2)
     partial_step(c2)
+    scan_end(1)
+    each(0, e1, lambda c: heads_of(c, last_step))
+    each(e1, e2, lambda c: heads_of(c, pair_step))
 
     def far_mix(*blocks_done):
         @pl.when(core != near)
@@ -760,7 +761,7 @@
         scan_close(3)
 
     far_mix(c2, c3)
-    each(e1, e3, lambda c: heads_of(c, pair_step))
+    each(e2, e3, lambda c: heads_of(c, pair_step))
     @pl.when(level < planes - 1)
     def _():
         scan_close(2)

time: 128 us -> 127 us (level)
  no operation moved by 1% of the time
where the time goes in v5:
time: 127 us
  Pallas kernels  127 us (100%)
    pallas_call x1, Pallas kernels, fused(): pl.pallas_call(functools.partial(kernel, blocks, chunks, PARTS), out_shap...  125 us

profile of v5, /device:TPU:0, one launch (start us, length us, event | category | flops | bytes accessed | tf_op | source)
XLA Modules:
  0.0 127.3 jit_solution(9660872215972862449)
XLA Ops:
  0.6 124.6 %shard_map.84 = (bf16[256,2048]{1,0:T(8,128)(2,1)S(1)}, bf16[256,2048]{1,0:T(8,128)(2,1)S(1)}, bf16[256,2048]{1,0:T(8,128)(2,1)S(1)}, bf16[256,2048]{1,0:T(8,128)(2,1)S(1)}) custom-call(bf16[256,2048]{1,0:T(8,128)(2,1)} %q_in.1, bf16[256,2048]{1,0:T(8,128)(2,1)} %k_in.1, bf16[256,2048]{1,0:T(8,128)(2,1)} %v_in.1, bf16[2048,256]{1,0:T(8,128)(2,1)} %w_ref.1, ...), custom_call_target="tpu_custom_call" | custom-call | tf_op jit(solution)/shard_map/pallas_call | solution.py:834
  125.3 2.0 %shard_map.85 = (bf16[256,2048]{1,0:T(8,128)(2,1)}, bf16[256,2048]{1,0:T(8,128)(2,1)}, bf16[256,2048]{1,0:T(8,128)(2,1)}, bf16[256,2048]{1,0:T(8,128)(2,1)}) custom-call(bf16[256,2048]{1,0:T(8,128)(2,1)S(1)} %get-tuple-element.8.refs_0_, bf16[256,2048]{1,0:T(8,128)(2,1)S(1)} %get-tuple-element.9.refs_1_, bf16[256,2048]{1,0:T(8,128)(2,1)S(1)} %get-tuple-element.10.refs_2_, ...), custom_call_target="tpu_custom_call" | custom-call | tf_op jit(solution)/shard_map/pallas_call | solution.py:804
